TPU v7x, 256 devices: a whole 4x4x8 slice. The times are simulated.
256 devices in a mesh: seq: 32 (over y, z_hi, core), head: 8 (over x, z_lo).
Axes of the slice: x: 4, y: 4, z: 8 (z_hi: 4, z_lo: 2; z = z_hi * 2 + z_lo), core: 2. Of those that a mesh axis runs over, the one named last changes fastest.
Arguments:
- tokens: bfloat16 [12288, 3072], P('seq'), may hold values from -70 to 70
- survive: int32 [12288], P('seq'), may hold values from 0 to 1, as said below
- norm_gain: float32 [3072], replicated, may hold values from 0.3 to 3
- w_qkv: bfloat16 [3072, 3, 3072], P(None, None, 'head'), may hold values from -0.109375 to 0.109375
- qk_gain: float32 [2, 24, 128], P(None, 'head'), may hold values from 0.5 to 2
- w_out: bfloat16 [3072, 3072], P('head'), may hold values from -0.109375 to 0.109375
Outputs:
- update: bfloat16 [12288, 3072], P('seq', 'head')
Inputs may be any that keep to these rules, and one draw needn't show every extreme that they name: `survive`: exactly 6144 tokens run in all. The 384 positions of one sequence shard hold anywhere from none to all 384 running tokens; in every draw some shard holds all 384 and some shard none.
All inputs are finite; a program needn't handle non-finite values.
Results may differ from a plain program's by a relative error of at most 0.015.
Values may be sent and summed in bfloat16 or wider, within the bound.
A program may use at most 128 MiB of HBM per device.

v0:
```python
import math

import jax
import jax.numpy as jnp
from jax import lax
from jax.sharding import PartitionSpec as P

epsilon = 1e-06
key_limit = 2048


def layer_norm(values, gain):
    center = values - jnp.mean(values, axis=-1, keepdims=True)
    spread = jnp.mean(center * center, axis=-1, keepdims=True)
    return center * lax.rsqrt(spread + epsilon) * gain


def project(source_tokens, norm_gain, w_qkv, qk_gain):
    width = source_tokens.shape[1]
    count_rows = source_tokens.shape[0]
    heads_here = qk_gain.shape[1]
    head_size = qk_gain.shape[2]
    inner_here = heads_here * head_size
    normed = layer_norm(source_tokens.astype(jnp.float32), norm_gain).astype(jnp.bfloat16)
    projected_output = jnp.dot(
        normed, w_qkv.reshape(width, 3 * inner_here), preferred_element_type=jnp.float32
    )
    query_rows = projected_output[:, :inner_here].reshape(count_rows, heads_here, head_size)
    running_key_rows = projected_output[:, inner_here : 2 * inner_here].reshape(
        count_rows, heads_here, head_size
    )
    query_rows = layer_norm(query_rows, qk_gain[0]).astype(jnp.bfloat16)
    running_key_rows = (
        layer_norm(running_key_rows, qk_gain[1])
        .astype(jnp.bfloat16)
        .reshape(count_rows, inner_here)
    )
    running_value_rows = projected_output[:, 2 * inner_here :].astype(jnp.bfloat16)
    return (query_rows, running_key_rows, running_value_rows)


def attend(query_rows, running_key_rows, running_value_rows, key_live):
    count_rows, heads_here, head_size = query_rows.shape
    score_scale = 1.0 / math.sqrt(head_size)
    shard_keys = running_key_rows.shape[0]

    def one_block(running, block_data):
        numerator, denominator = running
        block_keys, block_values, block_live = block_data
        width_keys = block_keys.shape[0]
        scores = (
            jnp.einsum(
                "qhd,khd->hqk",
                query_rows,
                block_keys.reshape(width_keys, heads_here, head_size),
                preferred_element_type=jnp.float32,
            )
            * score_scale
        )
        weights = jnp.exp(scores) * block_live.astype(jnp.float32)[None, None, :]
        denominator = denominator + jnp.sum(weights, axis=-1)
        numerator = numerator + jnp.einsum(
            "hqk,khd->qhd",
            weights.astype(jnp.bfloat16),
            block_values.reshape(width_keys, heads_here, head_size),
            preferred_element_type=jnp.float32,
        )
        return ((numerator, denominator), None)

    initial = (
        jnp.zeros(query_rows.shape, jnp.float32),
        jnp.zeros((heads_here, count_rows), jnp.float32),
    )
    running = initial
    piece_keys = lax.all_gather(running_key_rows, "seq", axis=0, tiled=True)
    piece_values = lax.all_gather(running_value_rows, "seq", axis=0, tiled=True)
    piece_live = lax.all_gather(key_live, "seq", axis=0, tiled=True)
    length = piece_keys.shape[0]
    shards_in = length // shard_keys
    most_shards = max(key_limit // shard_keys, 1)
    power_shards = 1 << most_shards.bit_length() - 1
    group_size = math.gcd(shards_in, power_shards)
    block_len = group_size * shard_keys
    blocks = length // block_len
    stacked = (
        piece_keys.reshape(blocks, block_len, piece_keys.shape[1]),
        piece_values.reshape(blocks, block_len, piece_values.shape[1]),
        piece_live.reshape(blocks, block_len),
    )
    running, unused = lax.scan(one_block, running, stacked)
    numerator, denominator = running
    attended_output = numerator / jnp.transpose(denominator)[:, :, None]
    return attended_output.astype(jnp.bfloat16).reshape(count_rows, heads_here * head_size)


def per_device(tokens, survive, norm_gain, w_qkv, qk_gain, w_out):
    key_live = survive.astype(jnp.bfloat16)
    query_rows, running_key_rows, running_value_rows = project(tokens, norm_gain, w_qkv, qk_gain)
    attended_output = attend(query_rows, running_key_rows, running_value_rows, key_live)
    branch_terms = jnp.dot(attended_output, w_out, preferred_element_type=jnp.float32)
    head_share = lax.psum_scatter(
        branch_terms.astype(jnp.bfloat16), "head", scatter_dimension=1, tiled=True
    ).astype(jnp.float32)
    update = jnp.where(survive[:, None] == 1, head_share, 0.0).astype(jnp.bfloat16)
    return update


def solution(mesh):
    placed = (
        P("seq", None),
        P("seq"),
        P(),
        P(None, None, "head"),
        P(None, "head", None),
        P("head", None),
    )
    return jax.shard_map(
        per_device, mesh=mesh, in_specs=placed, out_specs=P("seq", "head"), check_vma=False
    )
```

profile of v0, /device:TPU:32, one launch (start us, length us, event | category | flops | bytes accessed | tf_op | source)
XLA Modules:
  0.0 429.5 jit_solution(10876090292901378244)
XLA Ops:
  6.5 2.2 convert_reduce_fusion.1
  8.8 2.4 fusion.8
  11.2 10.3 %copy.34 = bf16[3072,3,384]{0,2,1:T(8,128)(2,1)} copy(bf16[3072,3,384]{2,0,1:T(8,128)(2,1)} %param.11) | data formatting | bytes 14155776 | tf_op args[3]
  21.5 7.1 %fusion.11 = f32[384,1152]{1,0:T(8,128)S(1)} fusion(bf16[3072,1152]{0,1:T(8,128)(2,1)} %bitcast.57, bf16[384,3072]{1,0:T(8,128)(2,1)} %param.8, f32[3072]{0:T(1024)S(1)} %copy-done.5, f32[384]{0:T(512)S(1)} %add_rsqrt_fusion.2, f32[384]{0:T(512)S(1)} %broadcast_multiply_fusion.2), kind=kOutput, calls=%fused_computation.21 | convolution fusion | flops 2723807232 | bytes 11222016 | tf_op jit(solution)/shard_map/dot_general | solution.py:25
  32.4 2.5 fusion.16
  35.0 1.8 slice.27
  38.3 47.4 %all-gather = bf16[32,1,384]{2,1,0:T(2,128)(2,1)S(1)} all-gather(bf16[1,1,384]{2,1,0:T(2,128)(2,1)S(1)} %reshape.89), channel_id=1, replica_groups=mesh['seq'=32,'head'=8] {'seq'}, dimensions={0}, use_global_device_ids=true | all-gather | bytes 25344 | tf_op jit(solution)/shard_map/all_gather | solution.py:77
  86.5 33.5 %all-gather.6.cloned.1.call-done = bf16[12288,384]{1,0:T(8,128)(2,1)} async-done(((bf16[384,384]{1,0:T(8,128)(2,1)}), bf16[12288,384]{1,0:T(8,128)(2,1)}) %all-gather.6.cloned.1.call-update) | async-done | bytes 9437200 | tf_op jit(solution)/shard_map/all_gather | solution.py:75
  120.0 84.6 %all-gather.4.cloned.1.call-done = bf16[12288,384]{1,0:T(8,128)(2,1)} async-done(((bf16[384,384]{1,0:T(8,128)(2,1)}), bf16[12288,384]{1,0:T(8,128)(2,1)}) %all-gather.4.cloned.1.call-update) | async-done | bytes 9437200 | tf_op jit(solution)/shard_map/all_gather | solution.py:76
  204.7 150.8 %while.13 = (s32[]{:T(128)}, f32[384,3,128]{0,2,1:T(8,128)}, f32[3,384]{1,0:T(4,128)}, bf16[8,1536,384]{2,1,0:T(8,128)(2,1)}, bf16[8,1536,384]{2,1,0:T(8,128)(2,...) while((s32[]{:T(128)}, f32[384,3,128]{0,2,1:T(8,128)}, ...), condition=%wide.region_8.9_spmd.clone, body=%wide.region_6.8_spmd.clone.sunk | while | flops 916884096 | bytes 27466860 | solution.py:90
  204.7 3.3 constant_dynamic-slice_fusion.3
  208.0 1.6 copy.54
  210.3 4.9 %bitcast_reduce_fusion.2 = (f32[3,384]{1,0:T(4,128)S(1)}, f32[3,1536,384]{2,1,0:T(8,128)}) fusion(f32[1536]{0:T(1024)S(1)} %convert_reduce_fusion.3, bf16[1536,3,128]{0,2,1:T(8,128)(2,1)S(1)} %bitcast.51, bf16[384,3,128]{2,0,1:T(8,128)(2,1)} %get-tuple-element.193), kind=kOutput, calls=%fused_computation.clone.1 | convolution fusion | flops 458292096 | bytes 8563200 | tf_op jit(solution)/shard_map/while/body/eval_jaxpr/qhd,khd->hqk/dot_general | solution.py:52
  215.3 1.6 copy.53
  216.9 5.4 %fusion.31 = f32[384,3,128]{0,2,1:T(8,128)} fusion(bf16[1536,3,128]{0,2,1:T(8,128)(2,1)S(1)} %bitcast.52, f32[3,1536,384]{2,1,0:T(8,128)} %get-tuple-element.168, f32[1536]{0:T(1024)S(1)} %convert_reduce_fusion.3, f32[384,3,128]{0,2,1:T(8,128)} %get-tuple-element.180, pred[]{:T(512)S(6)} %compare.3), kind=kOutput, calls=%fused_computation.7.clone.1 | convolution fusion | flops 458588160 | bytes 9443329 | tf_op jit(solution)/shard_map/while/body/eval_jaxpr/hqk,khd->qhd/dot_general | solution.py:62
  222.8 3.3 constant_dynamic-slice_fusion.3
  226.1 1.6 copy.54
  228.5 4.9 %bitcast_reduce_fusion.2 = (f32[3,384]{1,0:T(4,128)S(1)}, f32[3,1536,384]{2,1,0:T(8,128)}) fusion(f32[1536]{0:T(1024)S(1)} %convert_reduce_fusion.3, bf16[1536,3,128]{0,2,1:T(8,128)(2,1)S(1)} %bitcast.51, bf16[384,3,128]{2,0,1:T(8,128)(2,1)} %get-tuple-element.193), kind=kOutput, calls=%fused_computation.clone.1 | convolution fusion | flops 458292096 | bytes 8563200 | tf_op jit(solution)/shard_map/while/body/eval_jaxpr/qhd,khd->hqk/dot_general | solution.py:52
  233.4 1.6 copy.53
  235.0 5.5 %fusion.31 = f32[384,3,128]{0,2,1:T(8,128)} fusion(bf16[1536,3,128]{0,2,1:T(8,128)(2,1)S(1)} %bitcast.52, f32[3,1536,384]{2,1,0:T(8,128)} %get-tuple-element.168, f32[1536]{0:T(1024)S(1)} %convert_reduce_fusion.3, f32[384,3,128]{0,2,1:T(8,128)} %get-tuple-element.180, pred[]{:T(512)S(6)} %compare.3), kind=kOutput, calls=%fused_computation.7.clone.1 | convolution fusion | flops 458588160 | bytes 9443329 | tf_op jit(solution)/shard_map/while/body/eval_jaxpr/hqk,khd->qhd/dot_general | solution.py:62
  241.8 3.3 constant_dynamic-slice_fusion.3
  245.1 1.6 copy.54
  247.4 4.9 %bitcast_reduce_fusion.2 = (f32[3,384]{1,0:T(4,128)S(1)}, f32[3,1536,384]{2,1,0:T(8,128)}) fusion(f32[1536]{0:T(1024)S(1)} %convert_reduce_fusion.3, bf16[1536,3,128]{0,2,1:T(8,128)(2,1)S(1)} %bitcast.51, bf16[384,3,128]{2,0,1:T(8,128)(2,1)} %get-tuple-element.193), kind=kOutput, calls=%fused_computation.clone.1 | convolution fusion | flops 458292096 | bytes 8563200 | tf_op jit(solution)/shard_map/while/body/eval_jaxpr/qhd,khd->hqk/dot_general | solution.py:52
  252.4 1.6 copy.53
  253.9 5.5 %fusion.31 = f32[384,3,128]{0,2,1:T(8,128)} fusion(bf16[1536,3,128]{0,2,1:T(8,128)(2,1)S(1)} %bitcast.52, f32[3,1536,384]{2,1,0:T(8,128)} %get-tuple-element.168, f32[1536]{0:T(1024)S(1)} %convert_reduce_fusion.3, f32[384,3,128]{0,2,1:T(8,128)} %get-tuple-element.180, pred[]{:T(512)S(6)} %compare.3), kind=kOutput, calls=%fused_computation.7.clone.1 | convolution fusion | flops 458588160 | bytes 9443329 | tf_op jit(solution)/shard_map/while/body/eval_jaxpr/hqk,khd->qhd/dot_general | solution.py:62
  260.7 3.3 constant_dynamic-slice_fusion.3
  264.0 1.6 copy.54
  266.4 4.9 %bitcast_reduce_fusion.2 = (f32[3,384]{1,0:T(4,128)S(1)}, f32[3,1536,384]{2,1,0:T(8,128)}) fusion(f32[1536]{0:T(1024)S(1)} %convert_reduce_fusion.3, bf16[1536,3,128]{0,2,1:T(8,128)(2,1)S(1)} %bitcast.51, bf16[384,3,128]{2,0,1:T(8,128)(2,1)} %get-tuple-element.193), kind=kOutput, calls=%fused_computation.clone.1 | convolution fusion | flops 458292096 | bytes 8563200 | tf_op jit(solution)/shard_map/while/body/eval_jaxpr/qhd,khd->hqk/dot_general | solution.py:52
  271.3 1.6 copy.53
  272.9 5.5 %fusion.31 = f32[384,3,128]{0,2,1:T(8,128)} fusion(bf16[1536,3,128]{0,2,1:T(8,128)(2,1)S(1)} %bitcast.52, f32[3,1536,384]{2,1,0:T(8,128)} %get-tuple-element.168, f32[1536]{0:T(1024)S(1)} %convert_reduce_fusion.3, f32[384,3,128]{0,2,1:T(8,128)} %get-tuple-element.180, pred[]{:T(512)S(6)} %compare.3), kind=kOutput, calls=%fused_computation.7.clone.1 | convolution fusion | flops 458588160 | bytes 9443329 | tf_op jit(solution)/shard_map/while/body/eval_jaxpr/hqk,khd->qhd/dot_general | solution.py:62
  279.7 3.3 constant_dynamic-slice_fusion.3
  283.0 1.6 copy.54
  285.3 4.9 %bitcast_reduce_fusion.2 = (f32[3,384]{1,0:T(4,128)S(1)}, f32[3,1536,384]{2,1,0:T(8,128)}) fusion(f32[1536]{0:T(1024)S(1)} %convert_reduce_fusion.3, bf16[1536,3,128]{0,2,1:T(8,128)(2,1)S(1)} %bitcast.51, bf16[384,3,128]{2,0,1:T(8,128)(2,1)} %get-tuple-element.193), kind=kOutput, calls=%fused_computation.clone.1 | convolution fusion | flops 458292096 | bytes 8563200 | tf_op jit(solution)/shard_map/while/body/eval_jaxpr/qhd,khd->hqk/dot_general | solution.py:52
  290.3 1.6 copy.53
  291.8 5.5 %fusion.31 = f32[384,3,128]{0,2,1:T(8,128)} fusion(bf16[1536,3,128]{0,2,1:T(8,128)(2,1)S(1)} %bitcast.52, f32[3,1536,384]{2,1,0:T(8,128)} %get-tuple-element.168, f32[1536]{0:T(1024)S(1)} %convert_reduce_fusion.3, f32[384,3,128]{0,2,1:T(8,128)} %get-tuple-element.180, pred[]{:T(512)S(6)} %compare.3), kind=kOutput, calls=%fused_computation.7.clone.1 | convolution fusion | flops 458588160 | bytes 9443329 | tf_op jit(solution)/shard_map/while/body/eval_jaxpr/hqk,khd->qhd/dot_general | solution.py:62
  298.6 3.3 constant_dynamic-slice_fusion.3
  304.3 4.9 %bitcast_reduce_fusion.2 = (f32[3,384]{1,0:T(4,128)S(1)}, f32[3,1536,384]{2,1,0:T(8,128)}) fusion(f32[1536]{0:T(1024)S(1)} %convert_reduce_fusion.3, bf16[1536,3,128]{0,2,1:T(8,128)(2,1)S(1)} %bitcast.51, bf16[384,3,128]{2,0,1:T(8,128)(2,1)} %get-tuple-element.193), kind=kOutput, calls=%fused_computation.clone.1 | convolution fusion | flops 458292096 | bytes 8563200 | tf_op jit(solution)/shard_map/while/body/eval_jaxpr/qhd,khd->hqk/dot_general | solution.py:52
  310.8 5.5 %fusion.31 = f32[384,3,128]{0,2,1:T(8,128)} fusion(bf16[1536,3,128]{0,2,1:T(8,128)(2,1)S(1)} %bitcast.52, f32[3,1536,384]{2,1,0:T(8,128)} %get-tuple-element.168, f32[1536]{0:T(1024)S(1)} %convert_reduce_fusion.3, f32[384,3,128]{0,2,1:T(8,128)} %get-tuple-element.180, pred[]{:T(512)S(6)} %compare.3), kind=kOutput, calls=%fused_computation.7.clone.1 | convolution fusion | flops 458588160 | bytes 9443329 | tf_op jit(solution)/shard_map/while/body/eval_jaxpr/hqk,khd->qhd/dot_general | solution.py:62
  317.6 3.3 constant_dynamic-slice_fusion.3
  323.2 4.9 %bitcast_reduce_fusion.2 = (f32[3,384]{1,0:T(4,128)S(1)}, f32[3,1536,384]{2,1,0:T(8,128)}) fusion(f32[1536]{0:T(1024)S(1)} %convert_reduce_fusion.3, bf16[1536,3,128]{0,2,1:T(8,128)(2,1)S(1)} %bitcast.51, bf16[384,3,128]{2,0,1:T(8,128)(2,1)} %get-tuple-element.193), kind=kOutput, calls=%fused_computation.clone.1 | convolution fusion | flops 458292096 | bytes 8563200 | tf_op jit(solution)/shard_map/while/body/eval_jaxpr/qhd,khd->hqk/dot_general | solution.py:52
  329.7 5.5 %fusion.31 = f32[384,3,128]{0,2,1:T(8,128)} fusion(bf16[1536,3,128]{0,2,1:T(8,128)(2,1)S(1)} %bitcast.52, f32[3,1536,384]{2,1,0:T(8,128)} %get-tuple-element.168, f32[1536]{0:T(1024)S(1)} %convert_reduce_fusion.3, f32[384,3,128]{0,2,1:T(8,128)} %get-tuple-element.180, pred[]{:T(512)S(6)} %compare.3), kind=kOutput, calls=%fused_computation.7.clone.1 | convolution fusion | flops 458588160 | bytes 9443329 | tf_op jit(solution)/shard_map/while/body/eval_jaxpr/hqk,khd->qhd/dot_general | solution.py:62
  336.5 3.3 constant_dynamic-slice_fusion.3
  342.2 4.9 %bitcast_reduce_fusion.2 = (f32[3,384]{1,0:T(4,128)S(1)}, f32[3,1536,384]{2,1,0:T(8,128)}) fusion(f32[1536]{0:T(1024)S(1)} %convert_reduce_fusion.3, bf16[1536,3,128]{0,2,1:T(8,128)(2,1)S(1)} %bitcast.51, bf16[384,3,128]{2,0,1:T(8,128)(2,1)} %get-tuple-element.193), kind=kOutput, calls=%fused_computation.clone.1 | convolution fusion | flops 458292096 | bytes 8563200 | tf_op jit(solution)/shard_map/while/body/eval_jaxpr/qhd,khd->hqk/dot_general | solution.py:52
  347.1 1.6 copy.53
  348.7 5.5 %fusion.31 = f32[384,3,128]{0,2,1:T(8,128)} fusion(bf16[1536,3,128]{0,2,1:T(8,128)(2,1)S(1)} %bitcast.52, f32[3,1536,384]{2,1,0:T(8,128)} %get-tuple-element.168, f32[1536]{0:T(1024)S(1)} %convert_reduce_fusion.3, f32[384,3,128]{0,2,1:T(8,128)} %get-tuple-element.180, pred[]{:T(512)S(6)} %compare.3), kind=kOutput, calls=%fused_computation.7.clone.1 | convolution fusion | flops 458588160 | bytes 9443329 | tf_op jit(solution)/shard_map/while/body/eval_jaxpr/hqk,khd->qhd/dot_general | solution.py:62
  356.6 2.8 convolution_convert_fusion
  359.4 4.3 copy.44
  363.7 57.2 %reduce-scatter.4.cloned.1.call-done = bf16[384,384]{1,0:T(8,128)(2,1)} async-done(((bf16[3072,384]{1,0:T(8,128)(2,1)}), bf16[384,384]{1,0:T(8,128)(2,1)}) %reduce-scatter.4.cloned.1.call-update) | async-done | bytes 294928
  (70 shorter events, 32.9 us)
Async XLA Ops:
  6.5 350.0 %copy-start = (bf16[384,3072]{1,0:T(8,128)(2,1)S(1)}, bf16[384,3072]{1,0:T(8,128)(2,1)}, u32[]{:S(2)}) copy-start(bf16[384,3072]{1,0:T(8,128)(2,1)} %param.13) | copy-start | bytes 7077892
  6.5 113.5 %all-gather.6.cloned.1.call-start = ((), (), s32[]{:S(2)}) async-start(), calls=%async_computation.2 | async-start | bytes 9732096 | tf_op jit(solution)/shard_map/all_gather | solution.py:75
  11.2 10.3 %copy-start.5 = (f32[3072]{0:T(1024)S(1)}, f32[3072]{0:T(1024)}, u32[]{:S(2)}) copy-start(f32[3072]{0:T(1024)} %param.10) | copy-start | bytes 36868
  28.6 1.2 copy-start.1
  29.8 2.6 copy-start.4
  31.4 7.0 %copy-start.2 = (s32[384]{0:T(512)S(1)}, s32[384]{0:T(512)}, u32[]{:S(2)}) copy-start(s32[384]{0:T(512)} %param.9) | copy-start | bytes 4612
  34.9 169.7 %all-gather.4.cloned.1.call-start = ((), (), s32[]{:S(2)}) async-start(), calls=%async_computation.1 | async-start | bytes 9732096 | tf_op jit(solution)/shard_map/all_gather | solution.py:76
  36.8 384.1 %reduce-scatter.4.cloned.1.call-start = ((), (), s32[]{:S(2)}) async-start(), calls=%async_computation.3 | async-start | bytes 2654208
  359.4 4.3 %copy-start.3 = (s32[384]{0:T(512)S(1)}, s32[384]{0:T(512)}, u32[]{:S(2)}) copy-start(s32[384]{0:T(512)} %param.9) | copy-start | bytes 4612
Sparse Core Ops, SparseCore 0:
  35.0 84.9 all-gather.5
  122.6 82.0 all-gather.3
  363.8 57.0 reduce-scatter.3
where the time goes:
time: 434 us; the launch traced here: 429 us
  waiting for transfers between devices  175 us (40%)
  matrix products  93.2 us (21%)
  local copies, waits for them, and re-layouts  74.6 us (17%)
  blocking collectives  47.4 us (11%)
  other arithmetic  25.4 us (6%)
  between operations  13.3 us (3%)
    all_gather x1, waiting for transfers between devices, attend(): piece_values = lax.all_gather(running_value_rows, 'seq', axis=0, tiled=True)  84.6 us
    unnamed x4, waiting for transfers between devices  57.3 us
    dynamic_slice x24, local copies, waits for them, and re-layouts, attend(): running, unused = lax.scan(one_block, running, stacked)  51.6 us
    all_gather x1, blocking collectives, attend(): piece_live = lax.all_gather(key_live, 'seq', axis=0, tiled=True)  47.4 us
    dot_general x8, matrix products, one_block(): jnp.einsum('hqk,khd->qhd', weights.astype(jnp.bfloat16), block_values.res...  43.7 us
    dot_general x8, matrix products, one_block(): jnp.einsum('qhd,khd->hqk', query_rows, block_keys.reshape(width_keys, hea...  39.6 us
    all_gather x1, waiting for transfers between devices, attend(): piece_keys = lax.all_gather(running_key_rows, 'seq', axis=0, tiled=True)  33.5 us
    unnamed x18, local copies, waits for them, and re-layouts  17.9 us
  transfers between devices with their start and end apart: 3, of which 3 were waited for; matrix products, arithmetic and copies ran while one was open for 1% of the time, Pallas kernels for 0%

commit v1 on v0

v1 whole, which is shorter than its diff:
```python
import math

import jax
import jax.numpy as jnp
from jax import lax
from jax.experimental import pallas as pl
from jax.experimental.pallas import tpu as pltpu
from jax.sharding import PartitionSpec as P

epsilon = 1e-06
MESH = pl.DeviceIdType.MESH
f32, bf16 = jnp.float32, jnp.bfloat16

POS = 384
WIDTH = 3072
HEADS = 3
D = 128
CH = 3
RC = POS // CH
HALF = RC // 2


def column_of(row):
    return jnp.transpose(jnp.broadcast_to(row[0:1, :], (128, 128)))


def head_norm(x, gain):
    center = x - jnp.mean(x, axis=-1, keepdims=True)
    spread = jnp.mean(center * center, axis=-1, keepdims=True)
    return center * lax.rsqrt(spread + epsilon) * gain


def kernel(
    tok_hbm, sv_ref, ng_ref, w_hbm, qg_ref, wo_hbm, out_ref,
    tok, normed, w, wo, q, kv, lrow, lv, own, dn,
    zs, zra, zrb, zfm, zfp, zt, ds, dra, dfm, dfp, dt,
    att, xs, xown, xra, xrb, xfm, xfp, xt, zls, zlr,
    lsem, ssem, rsem,
):
    s = lax.axis_index("seq")
    hd = lax.axis_index("head")
    y, zh, co = s // 8, (s // 2) % 4, s % 2
    x, zl = hd // 2, hd % 2

    def seq_at(dy, dz, flip):
        c = (1 - co) if flip else co
        return {"seq": (((y + dy) % 4) * 4 + (zh + dz) % 4) * 2 + c}

    y_next, y_prev, sib = seq_at(1, 0, False), seq_at(3, 0, False), seq_at(0, 0, True)
    z_next, z_prev = seq_at(0, 1, False), seq_at(0, 3, False)
    x_next, x_prev = {"head": ((x + 1) % 4) * 2 + zl}, {"head": ((x + 3) % 4) * 2 + zl}
    z_pair = {"head": x * 2 + (1 - zl)}
    line = [
        (sib, 1), (y_next, 2), (seq_at(1, 0, True), 3), (y_prev, 4),
        (seq_at(3, 0, True), 5), (seq_at(2, 0, False), 6), (seq_at(2, 0, True), 7),
    ]

    loads = [pltpu.make_async_copy(tok_hbm, tok, lsem.at[0])]
    for j in range(3):
        loads.append(pltpu.make_async_copy(w_hbm.at[j], w.at[j], lsem.at[1 + j]))
    for r in range(4):
        for side in range(2):
            block = ((x + r) % 4) * 2 + (zl if side == 0 else 1 - zl)
            loads.append(
                pltpu.make_async_copy(
                    wo_hbm.at[:, pl.ds(pl.multiple_of(block * POS, 128), POS)],
                    wo.at[r, :, pl.ds(side * POS, POS)],
                    lsem.at[4 + 2 * r + side],
                )
            )
    for load in loads:
        load.start()

    barrier = pltpu.get_barrier_semaphore()
    peers = [p for p, _ in line] + [z_next, z_prev, x_next, x_prev, z_pair]
    for peer in peers:
        pl.semaphore_signal(barrier, inc=1, device_id=peer, device_id_type=MESH)

    count = [0]
    sent = []

    def message(src, dst, peer):
        i = count[0]
        count[0] += 1
        copy = pltpu.make_async_remote_copy(
            src_ref=src, dst_ref=dst, send_sem=ssem.at[i], recv_sem=rsem.at[i],
            device_id=peer, device_id_type=MESH,
        )
        sent.append(copy)
        return copy

    live = jnp.broadcast_to((sv_ref[...] == 1).astype(f32), (8, POS))
    lrow[0] = live
    for t in range(3):
        lv[0, t * 128 : (t + 1) * 128, :] = column_of(live[:, t * 128 : (t + 1) * 128]).astype(bf16)

    loads[0].wait()

    def norm_rows(i, carry):
        rows = pl.ds(pl.multiple_of(i * 16, 16), 16)
        v = tok[rows, :].astype(f32)
        center = v - jnp.mean(v, axis=-1, keepdims=True)
        spread = jnp.mean(center * center, axis=-1, keepdims=True)
        normed[rows, :] = (center * lax.rsqrt(spread + epsilon) * ng_ref[...]).astype(bf16)
        return carry

    lax.fori_loop(0, POS // 16, norm_rows, 0)

    loads[1].wait()
    projected = jnp.dot(normed[...], w[0], preferred_element_type=f32)
    score_scale = math.log2(math.e) / math.sqrt(D)
    for h in range(HEADS):
        gain = qg_ref[h, 0:1, :] * score_scale
        q[h, 0] = head_norm(projected[:, h * D : (h + 1) * D], gain).astype(bf16)

    pl.semaphore_wait(barrier, len(peers))

    live_msg = [message(lrow.at[0], lrow.at[slot], peer) for peer, slot in line]
    for m in live_msg:
        m.start()

    q_next = [message(q.at[h, 0], q.at[h, 1], z_next) for h in range(HEADS)]
    q_prev = [message(q.at[h, 0], q.at[h, 2], z_prev) for h in range(HEADS)]
    lo, hi = pl.ds(0, POS // 2), pl.ds(POS // 2, POS // 2)
    q_fwd_next = [message(q.at[h, 1, lo], q.at[h, 3, lo], z_next) for h in range(HEADS)]
    q_fwd_prev = [message(q.at[h, 2, hi], q.at[h, 3, hi], z_prev) for h in range(HEADS)]
    kv_next = [message(kv.at[h, 0], kv.at[h, 2], y_next) for h in range(HEADS)]
    kv_prev = [message(kv.at[h, 0], kv.at[h, 4], y_prev) for h in range(HEADS)]
    kv_fwd_next = [message(kv.at[h, 2, lo], kv.at[h, 6, lo], y_next) for h in range(HEADS)]
    kv_fwd_prev = [message(kv.at[h, 4, hi], kv.at[h, 6, hi], y_prev) for h in range(HEADS)]
    kv_sib = [[message(kv.at[h, 2 * r], kv.at[h, 2 * r + 1], sib) for r in range(4)] for h in range(HEADS)]

    def send_q(h):
        q_next[h].start()
        q_prev[h].start()

    def send_kv(h):
        kv_next[h].start()
        kv_prev[h].start()
        kv_sib[h][0].start()

    def forward_q(h):
        q_next[h].wait_recv()
        q_fwd_next[h].start()
        q_prev[h].wait_recv()
        q_fwd_prev[h].start()

    def forward_kv(h):
        kv_next[h].wait_recv()
        kv_fwd_next[h].start()
        kv_sib[h][1].start()
        kv_prev[h].wait_recv()
        kv_fwd_prev[h].start()
        kv_sib[h][2].start()

    def share_far(h):
        kv_fwd_next[h].wait_recv()
        kv_fwd_prev[h].wait_recv()
        kv_sib[h][3].start()

    def all_in(h):
        q_fwd_next[h].wait_recv()
        q_fwd_prev[h].wait_recv()
        for m in kv_sib[h]:
            m.wait_recv()

    def project_kv(h):
        cols = pl.ds(h * D, D)
        weights = jnp.concatenate([w[1, :, cols], w[2, :, cols]], axis=1)
        projected = jnp.dot(normed[...], weights, preferred_element_type=f32)
        kv[h, 0, :, 0:D] = head_norm(projected[:, :D], qg_ref[h, 1:2, :]).astype(bf16)
        kv[h, 0, :, D:] = (projected[:, D:] * lv[0].astype(f32)).astype(bf16)

    send_q(0)
    send_q(1)
    loads[2].wait()
    loads[3].wait()
    project_kv(0)
    send_kv(0)
    project_kv(1)
    send_kv(1)
    project_kv(2)

    for m, (_, slot) in zip(live_msg, line):
        m.wait_recv()
        for t in range(3):
            lv[slot, t * 128 : (t + 1) * 128, :] = column_of(lrow[slot, :, t * 128 : (t + 1) * 128]).astype(bf16)

    def unit(h, c):
        rows = pl.ds(c * RC, RC)
        queries = jnp.concatenate([q[h, slot, rows, :] for slot in range(4)], axis=0)
        keys = kv[h, :, :, 0:D].reshape(8 * POS, D)
        scores = lax.dot_general(queries, keys, (((1,), (1,)), ((), ())), preferred_element_type=f32)
        weights = jnp.exp2(scores).astype(bf16)
        values = jnp.concatenate([kv[h, :, :, D:].reshape(8 * POS, D), lv[...].reshape(8 * POS, D)], axis=1)
        acc = jnp.dot(weights, values, preferred_element_type=f32)
        own[h, c] = acc[0:RC, 0:D]
        for slot in range(1, 4):
            zs[h, c, slot - 1] = acc[slot * RC : (slot + 1) * RC, 0:D].astype(bf16)
        for slot in range(4):
            dn[h, c, slot] = acc[slot * RC : (slot + 1) * RC, D:]

    A, B = pl.ds(0, HALF), pl.ds(HALF, HALF)
    zmsg = {}
    for h in range(HEADS):
        for c in range(CH):
            zmsg[h, c] = [
                message(zs.at[h, c, 2, A], zra.at[h, c], z_next),
                message(zs.at[h, c, 2, B], zrb.at[h, c], z_prev),
                message(zs.at[h, c, 1, B], zfm.at[h, c, B], z_next),
                message(zs.at[h, c, 0, A], zfp.at[h, c, A], z_prev),
                message(zt.at[h, c, 0], zfm.at[h, c, A], z_next),
                message(zt.at[h, c, 1], zfp.at[h, c, B], z_prev),
            ]
    dmsg = [
        [
            message(ds.at[c, 2], dra.at[c], z_next),
            message(ds.at[c, 0], dfp.at[c], z_prev),
            message(dt.at[c], dfm.at[c], z_next),
        ]
        for c in range(CH)
    ]

    def z_first(h, c):
        for m in zmsg[h, c][:4]:
            m.start()
        if h == HEADS - 1:
            lane = lax.broadcasted_iota(jnp.int32, (RC, D), 1)
            for slot in range(1, 4):
                mixed = jnp.where(lane == 0, dn[0, c, slot], jnp.where(lane == 1, dn[1, c, slot], dn[2, c, slot]))
                ds[c, slot - 1] = jnp.transpose(mixed)[0:8, :]
            dmsg[c][0].start()
            dmsg[c][1].start()

    def z_relay(h, c):
        m = zmsg[h, c]
        m[0].wait_recv()
        zt[h, c, 0] = (zra[h, c].astype(f32) + zs[h, c, 1, 0:HALF].astype(f32)).astype(bf16)
        m[4].start()
        m[1].wait_recv()
        zt[h, c, 1] = (zrb[h, c].astype(f32) + zs[h, c, 0, HALF:].astype(f32)).astype(bf16)
        m[5].start()
        if h == HEADS - 1:
            dmsg[c][0].wait_recv()
            dt[c] = dra[c] + ds[c, 1]
            dmsg[c][2].start()

    xmsg = [
        [
            message(xs.at[c, 1, A], xra.at[c], x_next),
            message(xs.at[c, 1, B], xrb.at[c], x_prev),
            message(xs.at[c, 0, B], xfm.at[c, B], x_next),
            message(xs.at[c, 2, A], xfp.at[c, A], x_prev),
            message(xt.at[c, 0], xfm.at[c, A], x_next),
            message(xt.at[c, 1], xfp.at[c, B], x_prev),
        ]
        for c in range(CH)
    ]
    zlmsg = [message(zls.at[c], zlr.at[c], z_pair) for c in range(CH)]

    def attended(c):
        dmsg[c][1].wait_recv()
        dmsg[c][2].wait_recv()
        for h in range(HEADS):
            for m in zmsg[h, c][2:]:
                m.wait_recv()
            others = dfm[c, h : h + 1, :] + dfp[c, h : h + 1, :]
            den = dn[h, c, 0] + column_of(others)
            num = own[h, c] + zfm[h, c].astype(f32) + zfp[h, c].astype(f32)
            att[c, :, h * D : (h + 1) * D] = (num / den).astype(bf16)

    def x_first(c):
        a = att[c]
        for r in (2, 1, 3, 0):
            part = jnp.dot(a, wo[r], preferred_element_type=f32)
            if r == 0:
                xown[c] = part
            else:
                xs[c, r - 1] = part.astype(bf16)
            if r == 2:
                xmsg[c][0].start()
                xmsg[c][1].start()
            elif r == 1:
                xmsg[c][2].start()
            elif r == 3:
                xmsg[c][3].start()

    def x_relay(c):
        m = xmsg[c]
        m[0].wait_recv()
        xt[c, 0] = (xra[c].astype(f32) + xs[c, 0, 0:HALF].astype(f32)).astype(bf16)
        m[4].start()
        m[1].wait_recv()
        xt[c, 1] = (xrb[c].astype(f32) + xs[c, 2, HALF:].astype(f32)).astype(bf16)
        m[5].start()

    def x_final(c):
        for m in xmsg[c][2:]:
            m.wait_recv()
        total = xown[c] + xfm[c].astype(f32) + xfp[c].astype(f32)
        xown[c] = total
        zls[c] = total[:, POS:].astype(bf16)
        zlmsg[c].start()

    def finish(c):
        zlmsg[c].wait_recv()
        share = xown[c, :, 0:POS] + zlr[c].astype(f32)
        mask = lv[0, c * RC : (c + 1) * RC, :].astype(f32)
        mask = jnp.concatenate([mask] * (POS // D), axis=1)
        out_ref[c * RC : (c + 1) * RC, :] = jnp.where(mask > 0.5, share, 0.0).astype(bf16)

    forward_q(0)
    forward_kv(0)
    send_q(2)
    send_kv(2)
    forward_q(1)
    forward_kv(1)
    share_far(0)
    all_in(0)
    unit(0, 0)
    z_first(0, 0)
    forward_q(2)
    forward_kv(2)
    unit(0, 1)
    z_first(0, 1)
    z_relay(0, 0)
    share_far(1)
    unit(0, 2)
    z_first(0, 2)
    z_relay(0, 1)
    all_in(1)
    unit(1, 0)
    z_first(1, 0)
    z_relay(0, 2)
    share_far(2)
    unit(1, 1)
    z_first(1, 1)
    z_relay(1, 0)
    unit(1, 2)
    z_first(1, 2)
    z_relay(1, 1)
    all_in(2)
    unit(2, 0)
    z_first(2, 0)
    z_relay(1, 2)
    unit(2, 1)
    z_first(2, 1)
    z_relay(2, 0)
    for load in loads[4:]:
        load.wait()
    unit(2, 2)
    z_first(2, 2)
    z_relay(2, 1)
    attended(0)
    x_first(0)
    z_relay(2, 2)
    attended(1)
    x_first(1)
    x_relay(0)
    attended(2)
    x_first(2)
    x_relay(1)
    x_final(0)
    x_relay(2)
    x_final(1)
    finish(0)
    x_final(2)
    finish(1)
    finish(2)
    for copy in sent:
        copy.wait_send()


MESSAGES = 7 + 12 + 24 + 54 + 9 + 18 + 3


def per_device(tokens, survive, norm_gain, w_qkv, qk_gain, w_out):
    vmem = lambda *shape: pltpu.VMEM(shape, bf16)
    vmem32 = lambda *shape: pltpu.VMEM(shape, f32)
    units = (HEADS, CH)
    scratch = [
        vmem(POS, WIDTH), vmem(POS, WIDTH), vmem(3, WIDTH, POS), vmem(4, POS, 2 * POS),
        vmem(HEADS, 4, POS, D), vmem(HEADS, 8, POS, 2 * D), vmem32(8, 8, POS), vmem(8, POS, D),
        vmem32(*units, RC, D), vmem32(*units, 4, RC, D),
        vmem(*units, 3, RC, D), vmem(*units, HALF, D), vmem(*units, HALF, D),
        vmem(*units, RC, D), vmem(*units, RC, D), vmem(*units, 2, HALF, D),
        vmem32(CH, 3, 8, RC), vmem32(CH, 8, RC), vmem32(CH, 8, RC), vmem32(CH, 8, RC), vmem32(CH, 8, RC),
        vmem(CH, RC, POS), vmem(CH, 3, RC, 2 * POS), vmem32(CH, RC, 2 * POS),
        vmem(CH, HALF, 2 * POS), vmem(CH, HALF, 2 * POS), vmem(CH, RC, 2 * POS), vmem(CH, RC, 2 * POS),
        vmem(CH, 2, HALF, 2 * POS), vmem(CH, RC, POS), vmem(CH, RC, POS),
        pltpu.SemaphoreType.DMA((12,)),
        pltpu.SemaphoreType.DMA((MESSAGES,)),
        pltpu.SemaphoreType.DMA((MESSAGES,)),
    ]
    in_hbm = pl.BlockSpec(memory_space=pl.ANY)
    in_vmem = pl.BlockSpec(memory_space=pltpu.VMEM)
    return pl.pallas_call(
        kernel,
        out_shape=jax.ShapeDtypeStruct((POS, POS), bf16),
        in_specs=[in_hbm, in_vmem, in_vmem, in_hbm, in_vmem, in_hbm],
        out_specs=in_vmem,
        scratch_shapes=scratch,
        compiler_params=pltpu.CompilerParams(
            collective_id=0, has_side_effects=True, vmem_limit_bytes=60 * 2**20
        ),
        name="branch",
    )(
        tokens,
        survive.reshape(1, POS),
        norm_gain.reshape(1, WIDTH),
        jnp.transpose(w_qkv, (1, 0, 2)),
        jnp.transpose(qk_gain, (1, 0, 2)),
        w_out,
    )


def solution(mesh):
    placed = (
        P("seq", None),
        P("seq"),
        P(),
        P(None, None, "head"),
        P(None, "head", None),
        P("head", None),
    )
    return jax.shard_map(
        per_device, mesh=mesh, in_specs=placed, out_specs=P("seq", "head"), check_vma=False
    )
```

time: 434 us -> 92.5 us (0.21)
  waiting for transfers between devices: 175 us -> 0 us
  matrix products: 93.2 us -> 0 us
  Pallas kernels: 0 us -> 88.8 us
  local copies, waits for them, and re-layouts: 74.6 us -> 2.95 us
  blocking collectives: 47.4 us -> 0 us
  other arithmetic: 25.4 us -> 0 us
  between operations: 13.3 us -> 0.01 us
    all_gather x2 -> x0, waiting for transfers between devices: 118 us -> none  [the longest x1 84.6 us: attend(): piece_values = lax.all_gather(running_value_rows, 'seq', axis=0, tiled=True)]
    dot_general x18 -> x0, matrix products: 93.2 us -> none  [the longest x8 43.7 us: one_block(): jnp.einsum('hqk,khd->qhd', weights.astype(jnp.bfloat16), block_values.res...]
    pallas_call x0 -> x1, Pallas kernels: none -> 88.8 us  [per_device(): pl.pallas_call(kernel, out_shape=jax.ShapeDtypeStruct((POS, POS), bf16),...]
    unnamed x4 -> x0, waiting for transfers between devices: 57.3 us -> none
    dynamic_slice x24 -> x0, local copies, waits for them, and re-layouts: 51.6 us -> none  [attend(): running, unused = lax.scan(one_block, running, stacked)]
    all_gather x1 -> x0, blocking collectives: 47.4 us -> none  [attend(): piece_live = lax.all_gather(key_live, 'seq', axis=0, tiled=True)]
    unnamed x18 -> x1, local copies, waits for them, and re-layouts: 17.9 us -> 1.71 us
    add x8 -> x0, other arithmetic: 9.62 us -> none  [one_block(): denominator = denominator + jnp.sum(weights, axis=-1)]
  transfers between devices with their start and end apart: 3 -> 0, of which waited for: 3 -> 0; matrix products, arithmetic and copies ran while one was open for 1% -> 0% of each run, Pallas kernels for 0% -> 0%
where the time goes in v1:
time: 92.5 us; the launch traced here: 91.8 us
  Pallas kernels  88.8 us (96%)
  local copies, waits for them, and re-layouts  2.95 us (3%)
    pallas_call x1, Pallas kernels, per_device(): pl.pallas_call(kernel, out_shape=jax.ShapeDtypeStruct((POS, POS), bf16),...  88.8 us

profile of v1, /device:TPU:32, one launch (start us, length us, event | category | flops | bytes accessed | tf_op | source)
XLA Modules:
  0.0 91.8 jit_solution(4119602127007080677)
XLA Ops:
  0.0 1.2 %reshape.6.sv_ref = s32[1,384]{1,0:T(1,128)} reshape(s32[384]{0:T(512)} %param.7) | data formatting | bytes 3072 | tf_op jit(solution)/shard_map/reshape | solution.py:409
  1.2 88.8 %branch.1 = bf16[384,384]{1,0:T(8,128)(2,1)} custom-call(bf16[384,3072]{1,0:T(8,128)(2,1)} %tok_hbm.1, s32[1,384]{1,0:T(1,128)} %reshape.6.sv_ref, f32[1,3072]{1,0:T(1,128)} %bitcast.4, bf16[3,3072,384]{2,1,0:T(8,128)(2,1)} %bitcast.3, f32[3,2,128]{2,1,0:T(2,128)} %bitcast.5, bf16[384,3072]{1,0:T(8,128)(2,1)} %wo_hbm.1), custom_call_target="tpu_custom_call" | custom-call | tf_op jit(solution)/shard_map/branch/pallas_call | solution.py:397
  90.1 1.7 %copy.8 = bf16[384,384]{1,0:T(8,128)(2,1)} copy(bf16[384,384]{1,0:T(8,128)(2,1)} %branch.1) | data formatting | bytes 589824

commit v2 on v1

v2 whole, which is shorter than its diff:
```python
import math

import jax
import jax.numpy as jnp
from jax import lax
from jax.experimental import pallas as pl
from jax.experimental.pallas import tpu as pltpu
from jax.sharding import PartitionSpec as P

epsilon = 1e-06
MESH = pl.DeviceIdType.MESH
f32, bf16 = jnp.float32, jnp.bfloat16

POS = 384
WIDTH = 3072
HEADS = 3
D = 128
CH = 3
RC = POS // CH
HALF = RC // 2


def column_of(row):
    return jnp.transpose(jnp.broadcast_to(row, (128, 128)))


def head_norm(x, gain):
    center = x - jnp.mean(x, axis=-1, keepdims=True)
    spread = jnp.mean(center * center, axis=-1, keepdims=True)
    return center * lax.rsqrt(spread + epsilon) * gain


def kernel(
    tok_hbm, sv_ref, ng_ref, w_hbm, qg_ref, wo_hbm, out_ref,
    tok, normed, w, wo, q, kv, lrow, lv, own, dn,
    zs, zra, zrb, zfm, zfp, zt, ds, dra, dfm, dfp, dt,
    xa, total, zls, zlr,
    lsem, ssem, rsem,
):
    s = lax.axis_index("seq")
    hd = lax.axis_index("head")
    y, zh, co = s // 8, (s // 2) % 4, s % 2
    x, zl = hd // 2, hd % 2

    def seq_at(dy, dz, flip):
        c = (1 - co) if flip else co
        return {"seq": (((y + dy) % 4) * 4 + (zh + dz) % 4) * 2 + c}

    y_next, y_prev, sib = seq_at(1, 0, False), seq_at(3, 0, False), seq_at(0, 0, True)
    z_next, z_prev = seq_at(0, 1, False), seq_at(0, 3, False)
    x_next, x_prev, x_far = ({"head": ((x + dx) % 4) * 2 + zl} for dx in (1, 3, 2))
    z_pair = {"head": x * 2 + (1 - zl)}
    line = [
        (sib, 1), (y_next, 2), (seq_at(1, 0, True), 3), (y_prev, 4),
        (seq_at(3, 0, True), 5), (seq_at(2, 0, False), 6), (seq_at(2, 0, True), 7),
    ]

    token_loads = []
    for c in range(CH):
        rows = pl.ds(c * RC, RC)
        token_loads.append(pltpu.make_async_copy(tok_hbm.at[rows], tok.at[rows], lsem.at[c]))
    w_loads = [pltpu.make_async_copy(w_hbm.at[j], w.at[j], lsem.at[CH + j]) for j in range(3)]
    x_cols = lambda dx: pl.ds(pl.multiple_of(((x + dx) % 4) * 2 * POS, 128), 2 * POS)
    wo_load = pltpu.make_async_copy(wo_hbm.at[:, x_cols(0)], wo.at[0], lsem.at[CH + 3])
    loads = token_loads + w_loads + [wo_load]
    for load in loads:
        load.start()

    barrier = pltpu.get_barrier_semaphore()
    peers = [p for p, _ in line] + [z_next, z_prev, x_next, x_prev, x_far, z_pair]
    for peer in peers:
        pl.semaphore_signal(barrier, inc=1, device_id=peer, device_id_type=MESH)

    count = [0]
    sent = []

    def message(src, dst, peer):
        i = count[0]
        count[0] += 1
        copy = pltpu.make_async_remote_copy(
            src_ref=src, dst_ref=dst, send_sem=ssem.at[i], recv_sem=rsem.at[i],
            device_id=peer, device_id_type=MESH,
        )
        sent.append(copy)
        return copy

    lrow[0] = jnp.zeros((8, 128), f32)
    lrow[0, 0:CH, :] = (sv_ref[...] == 1).astype(f32)

    def spread_live(slot):
        for t in range(CH):
            lv[slot, t * RC : (t + 1) * RC, :] = column_of(lrow[slot, t : t + 1, :]).astype(bf16)

    spread_live(0)

    def norm_rows(i, carry):
        rows = pl.ds(pl.multiple_of(i * 16, 16), 16)
        v = tok[rows, :].astype(f32)
        center = v - jnp.mean(v, axis=-1, keepdims=True)
        spread = jnp.mean(center * center, axis=-1, keepdims=True)
        normed[rows, :] = (center * lax.rsqrt(spread + epsilon) * ng_ref[...]).astype(bf16)
        return carry

    for c in range(CH):
        token_loads[c].wait()
        lax.fori_loop(c * RC // 16, (c + 1) * RC // 16, norm_rows, 0)

    w_loads[0].wait()
    projected = jnp.dot(normed[...], w[0], preferred_element_type=f32)
    score_scale = math.log2(math.e) / math.sqrt(D)
    for h in range(HEADS):
        gain = qg_ref[h, 0:1, :] * score_scale
        q[h, 0] = head_norm(projected[:, h * D : (h + 1) * D], gain).astype(bf16)

    pl.semaphore_wait(barrier, len(peers))

    live_msg = [message(lrow.at[0], lrow.at[slot], peer) for peer, slot in line]
    core_rows = pl.ds(pl.multiple_of(co * (POS // 2), 16), POS // 2)
    wo_msg = [
        message(wo_hbm.at[core_rows, x_cols(dx)], wo.at[r, core_rows], peer)
        for dx, r, peer in ((1, 1, x_next), (3, 2, x_prev), (2, 3, x_far))
    ]
    wo_sib = [message(wo.at[r, core_rows], wo.at[r, core_rows], sib) for r in (1, 2, 3)]
    for m in live_msg + wo_msg:
        m.start()

    q_next = [message(q.at[h, 0], q.at[h, 1], z_next) for h in range(HEADS)]
    q_prev = [message(q.at[h, 0], q.at[h, 2], z_prev) for h in range(HEADS)]
    lo, hi = pl.ds(0, POS // 2), pl.ds(POS // 2, POS // 2)
    q_fwd_next = [message(q.at[h, 1, lo], q.at[h, 3, lo], z_next) for h in range(HEADS)]
    q_fwd_prev = [message(q.at[h, 2, hi], q.at[h, 3, hi], z_prev) for h in range(HEADS)]
    kv_next = [message(kv.at[h, 0], kv.at[h, 2], y_next) for h in range(HEADS)]
    kv_prev = [message(kv.at[h, 0], kv.at[h, 4], y_prev) for h in range(HEADS)]
    kv_fwd_next = [message(kv.at[h, 2, lo], kv.at[h, 6, lo], y_next) for h in range(HEADS)]
    kv_fwd_prev = [message(kv.at[h, 4, hi], kv.at[h, 6, hi], y_prev) for h in range(HEADS)]
    kv_sib = [[message(kv.at[h, 2 * r], kv.at[h, 2 * r + 1], sib) for r in range(4)] for h in range(HEADS)]

    def send_q(h):
        q_next[h].start()
        q_prev[h].start()

    def send_kv(h):
        kv_next[h].start()
        kv_prev[h].start()
        kv_sib[h][0].start()

    def forward_q(h):
        q_next[h].wait_recv()
        q_fwd_next[h].start()
        q_prev[h].wait_recv()
        q_fwd_prev[h].start()

    def forward_kv(h):
        kv_next[h].wait_recv()
        kv_fwd_next[h].start()
        kv_sib[h][1].start()
        kv_prev[h].wait_recv()
        kv_fwd_prev[h].start()
        kv_sib[h][2].start()

    def share_far(h):
        kv_fwd_next[h].wait_recv()
        kv_fwd_prev[h].wait_recv()
        kv_sib[h][3].start()

    def all_in(h):
        q_fwd_next[h].wait_recv()
        q_fwd_prev[h].wait_recv()
        for m in kv_sib[h]:
            m.wait_recv()

    def project_kv(h):
        cols = pl.ds(h * D, D)
        weights = jnp.concatenate([w[1, :, cols], w[2, :, cols]], axis=1)
        projected = jnp.dot(normed[...], weights, preferred_element_type=f32)
        kv[h, 0, :, 0:D] = head_norm(projected[:, :D], qg_ref[h, 1:2, :]).astype(bf16)
        kv[h, 0, :, D:] = (projected[:, D:] * lv[0].astype(f32)).astype(bf16)

    send_q(0)
    send_q(1)
    w_loads[1].wait()
    w_loads[2].wait()
    project_kv(0)
    send_kv(0)
    project_kv(1)
    send_kv(1)
    project_kv(2)

    for m, (_, slot) in zip(live_msg, line):
        m.wait_recv()
        spread_live(slot)

    def unit(h, c):
        rows = pl.ds(c * RC, RC)
        queries = jnp.concatenate([q[h, slot, rows, :] for slot in range(4)], axis=0)
        keys = kv[h, :, :, 0:D].reshape(8 * POS, D)
        scores = lax.dot_general(queries, keys, (((1,), (1,)), ((), ())), preferred_element_type=f32)
        weights = jnp.exp2(scores).astype(bf16)
        values = jnp.concatenate([kv[h, :, :, D:].reshape(8 * POS, D), lv[...].reshape(8 * POS, D)], axis=1)
        acc = jnp.dot(weights, values, preferred_element_type=f32)
        own[h, c] = acc[0:RC, 0:D]
        for slot in range(1, 4):
            zs[h, c, slot - 1] = acc[slot * RC : (slot + 1) * RC, 0:D].astype(bf16)
        for slot in range(4):
            dn[h, c, slot] = acc[slot * RC : (slot + 1) * RC, D:]

    A, B = pl.ds(0, HALF), pl.ds(HALF, HALF)
    zmsg = {}
    for h in range(HEADS):
        for c in range(CH):
            zmsg[h, c] = [
                message(zs.at[h, c, 2, A], zra.at[h, c], z_next),
                message(zs.at[h, c, 2, B], zrb.at[h, c], z_prev),
                message(zs.at[h, c, 1, B], zfm.at[h, c, B], z_next),
                message(zs.at[h, c, 0, A], zfp.at[h, c, A], z_prev),
                message(zt.at[h, c, 0], zfm.at[h, c, A], z_next),
                message(zt.at[h, c, 1], zfp.at[h, c, B], z_prev),
            ]
    dmsg = {}
    for h in range(HEADS):
        for c in range(CH):
            dmsg[h, c] = [
                message(ds.at[h, c, 2], dra.at[h, c], z_next),
                message(ds.at[h, c, 0], dfp.at[h, c], z_prev),
                message(dt.at[h, c], dfm.at[h, c], z_next),
            ]

    def z_first(h, c):
        for m in zmsg[h, c][:4]:
            m.start()
        lane = lax.broadcasted_iota(jnp.int32, (RC, D), 1)
        mixed = jnp.where(lane == 0, dn[h, c, 1], jnp.where(lane == 1, dn[h, c, 2], dn[h, c, 3]))
        rows = jnp.transpose(mixed)[0:8, :]
        for i in range(3):
            ds[h, c, i] = jnp.broadcast_to(rows[i : i + 1, :], (8, RC))
        dmsg[h, c][0].start()
        dmsg[h, c][1].start()

    def z_relay(h, c):
        m = zmsg[h, c]
        m[0].wait_recv()
        zt[h, c, 0] = (zra[h, c].astype(f32) + zs[h, c, 1, 0:HALF].astype(f32)).astype(bf16)
        m[4].start()
        m[1].wait_recv()
        zt[h, c, 1] = (zrb[h, c].astype(f32) + zs[h, c, 0, HALF:].astype(f32)).astype(bf16)
        m[5].start()
        d = dmsg[h, c]
        d[0].wait_recv()
        dt[h, c] = dra[h, c] + ds[h, c, 1]
        d[2].start()

    xmsg = {}
    for h in range(HEADS):
        for c in range(CH):
            xmsg[h, c] = [
                message(xa.at[0, h, c], xa.at[1, h, c], x_next),
                message(xa.at[0, h, c], xa.at[2, h, c], x_prev),
                message(xa.at[1, h, c, A], xa.at[3, h, c, A], x_next),
                message(xa.at[2, h, c, B], xa.at[3, h, c, B], x_prev),
            ]
    zlmsg = [message(zls.at[c], zlr.at[c], z_pair) for c in range(CH)]

    def attended(h, c):
        dmsg[h, c][1].wait_recv()
        dmsg[h, c][2].wait_recv()
        for m in zmsg[h, c][2:]:
            m.wait_recv()
        den = dn[h, c, 0] + column_of(dfm[h, c, 0:1, :] + dfp[h, c, 0:1, :])
        num = own[h, c] + zfm[h, c].astype(f32) + zfp[h, c].astype(f32)
        xa[0, h, c] = (num / den).astype(bf16)
        xmsg[h, c][0].start()
        xmsg[h, c][1].start()

    def x_forward(h, c):
        m = xmsg[h, c]
        m[0].wait_recv()
        m[2].start()
        m[1].wait_recv()
        m[3].start()

    def project_out(c):
        for h in range(HEADS):
            xmsg[h, c][2].wait_recv()
            xmsg[h, c][3].wait_recv()
        rows = jnp.concatenate([xa[r, h, c] for r in range(4) for h in range(HEADS)], axis=1)
        weights = wo[...].reshape(4 * POS, 2 * POS)
        total[c] = jnp.dot(rows, weights, preferred_element_type=f32)
        other = pl.ds(pl.multiple_of((1 - zl) * POS, 128), POS)
        zls[c] = total[c, :, other].astype(bf16)
        zlmsg[c].start()

    def finish(c):
        zlmsg[c].wait_recv()
        mine = pl.ds(pl.multiple_of(zl * POS, 128), POS)
        out_ref[c * RC : (c + 1) * RC, :] = (total[c, :, mine] + zlr[c].astype(f32)).astype(bf16)

    def share_weights():
        for m, share in zip(wo_msg, wo_sib):
            m.wait_recv()
            share.start()

    steps = [(h, c) for h in range(HEADS) for c in range(CH)]

    def after(u):
        z_first(*steps[u])
        if u >= 2:
            z_relay(*steps[u - 2])
        if u >= 4:
            attended(*steps[u - 4])
        if u >= 5:
            x_forward(*steps[u - 5])

    def step(u):
        unit(*steps[u])
        after(u)

    forward_q(0)
    forward_kv(0)
    send_q(2)
    send_kv(2)
    forward_q(1)
    forward_kv(1)
    share_far(0)
    all_in(0)
    step(0)
    forward_q(2)
    forward_kv(2)
    step(1)
    share_far(1)
    step(2)
    all_in(1)
    step(3)
    share_far(2)
    step(4)
    share_weights()
    step(5)
    all_in(2)
    step(6)
    step(7)
    step(8)
    z_relay(*steps[7])
    attended(*steps[5])
    z_relay(*steps[8])
    x_forward(*steps[4])
    wo_load.wait()
    for m in wo_sib:
        m.wait_recv()
    attended(*steps[6])
    x_forward(*steps[5])
    attended(*steps[7])
    x_forward(*steps[6])
    attended(*steps[8])
    project_out(0)
    x_forward(*steps[7])
    project_out(1)
    x_forward(*steps[8])
    project_out(2)
    for c in range(CH):
        finish(c)
    for copy in sent:
        copy.wait_send()


MESSAGES = 7 + 6 + 12 + 24 + 54 + 27 + 36 + 3


def per_device(tokens, survive, norm_gain, w_qkv, qk_gain, w_out):
    vmem = lambda *shape: pltpu.VMEM(shape, bf16)
    vmem32 = lambda *shape: pltpu.VMEM(shape, f32)
    units = (HEADS, CH)
    scratch = [
        vmem(POS, WIDTH), vmem(POS, WIDTH), vmem(3, WIDTH, POS), vmem(4, POS, 2 * POS),
        vmem(HEADS, 4, POS, D), vmem(HEADS, 8, POS, 2 * D), vmem32(8, 8, 128), vmem(8, POS, D),
        vmem32(*units, RC, D), vmem32(*units, 4, RC, D),
        vmem(*units, 3, RC, D), vmem(*units, HALF, D), vmem(*units, HALF, D),
        vmem(*units, RC, D), vmem(*units, RC, D), vmem(*units, 2, HALF, D),
        vmem32(*units, 3, 8, RC), vmem32(*units, 8, RC), vmem32(*units, 8, RC), vmem32(*units, 8, RC),
        vmem32(*units, 8, RC),
        vmem(4, *units, RC, D), vmem32(CH, RC, 2 * POS), vmem(CH, RC, POS), vmem(CH, RC, POS),
        pltpu.SemaphoreType.DMA((CH + 4,)),
        pltpu.SemaphoreType.DMA((MESSAGES,)),
        pltpu.SemaphoreType.DMA((MESSAGES,)),
    ]
    in_hbm = pl.BlockSpec(memory_space=pl.ANY)
    in_vmem = pl.BlockSpec(memory_space=pltpu.VMEM)
    share = pl.pallas_call(
        kernel,
        out_shape=jax.ShapeDtypeStruct((POS, POS), bf16),
        in_specs=[in_hbm, in_vmem, in_vmem, in_hbm, in_vmem, in_hbm],
        out_specs=in_vmem,
        scratch_shapes=scratch,
        compiler_params=pltpu.CompilerParams(
            collective_id=0, has_side_effects=True, vmem_limit_bytes=60 * 2**20
        ),
        name="branch",
    )(
        tokens,
        survive.reshape(CH, RC),
        norm_gain.reshape(1, WIDTH),
        jnp.transpose(w_qkv, (1, 0, 2)),
        jnp.transpose(qk_gain, (1, 0, 2)),
        w_out,
    )
    return jnp.where(survive[:, None] == 1, share, jnp.zeros_like(share))


def solution(mesh):
    placed = (
        P("seq", None),
        P("seq"),
        P(),
        P(None, None, "head"),
        P(None, "head", None),
        P("head", None),
    )
    return jax.shard_map(
        per_device, mesh=mesh, in_specs=placed, out_specs=P("seq", "head"), check_vma=False
    )
```

time: 92.5 us -> 87.7 us (0.948)
  Pallas kernels: 88.8 us -> 85 us
  local copies, waits for them, and re-layouts: 2.95 us -> 0 us
  other arithmetic: 0 us -> 2.49 us
    pallas_call x1, Pallas kernels: 88.8 us -> 85 us  [per_device(): pl.pallas_call(kernel, out_shape=jax.ShapeDtypeStruct((POS, POS), bf16),...]
    select_n x0 -> x1, other arithmetic: none -> 1.8 us  [per_device(): return jnp.where(survive[:, None] == 1, share, jnp.zeros_like(share))]
    unnamed x1 -> x0, local copies, waits for them, and re-layouts: 1.71 us -> none
    reshape x1 -> x0, local copies, waits for them, and re-layouts: 1.24 us -> none  [per_device(): survive.reshape(1, POS)]
where the time goes in v2:
time: 87.7 us; the launch traced here: 87.5 us
  Pallas kernels  85 us (97%)
  other arithmetic  2.49 us (3%)
    pallas_call x1, Pallas kernels, per_device(): pl.pallas_call(kernel, out_shape=jax.ShapeDtypeStruct((POS, POS), bf16),...  85 us
    select_n x1, other arithmetic, per_device(): return jnp.where(survive[:, None] == 1, share, jnp.zeros_like(share))  1.8 us

profile of v2, /device:TPU:32, one launch (start us, length us, event | category | flops | bytes accessed | tf_op | source)
XLA Modules:
  0.0 87.5 jit_solution(14549176066999347389)
XLA Ops:
  0.0 0.7 broadcast_compare_fusion
  0.7 85.0 %branch.1 = bf16[384,384]{1,0:T(8,128)(2,1)} custom-call(bf16[384,3072]{1,0:T(8,128)(2,1)} %tok_hbm.1, s32[3,128]{1,0:T(4,128)} %bitcast.6, f32[1,3072]{1,0:T(1,128)} %bitcast.5, bf16[3,3072,384]{2,1,0:T(8,128)(2,1)} %bitcast.4, f32[3,2,128]{2,1,0:T(2,128)} %bitcast.7, bf16[384,3072]{1,0:T(8,128)(2,1)} %wo_hbm.1), custom_call_target="tpu_custom_call" | custom-call | tf_op jit(solution)/shard_map/branch/pallas_call | solution.py:386
  85.7 1.8 %broadcast_select_fusion = bf16[384,384]{1,0:T(8,128)(2,1)} fusion(bf16[384,384]{1,0:T(8,128)(2,1)} %branch.1, pred[384]{0:T(512)(128)(4,1)S(1)} %broadcast_compare_fusion), kind=kLoop, calls=%fused_computation | loop fusion | flops 147456 | bytes 590208 | tf_op jit(solution)/shard_map/jit(_where)/select_n | solution.py:404

commit v3 on v2

--- a/solution.py
+++ b/solution.py
@@ -18,6 +18,7 @@
 CH = 3
 RC = POS // CH
 HALF = RC // 2
+DIRECT = [(2, 2)]
 
 
 def column_of(row):
@@ -33,7 +34,7 @@
 def kernel(
     tok_hbm, sv_ref, ng_ref, w_hbm, qg_ref, wo_hbm, out_ref,
     tok, normed, w, wo, q, kv, lrow, lv, own, dn,
-    zs, zra, zrb, zfm, zfp, zt, ds, dra, dfm, dfp, dt,
+    zs, zra, zrb, zfm, zfp, zff, zt, ds, dra, dfm, dfp, dff, dt,
     xa, total, zls, zlr,
     lsem, ssem, rsem,
 ):
@@ -47,7 +48,7 @@
         return {"seq": (((y + dy) % 4) * 4 + (zh + dz) % 4) * 2 + c}
 
     y_next, y_prev, sib = seq_at(1, 0, False), seq_at(3, 0, False), seq_at(0, 0, True)
-    z_next, z_prev = seq_at(0, 1, False), seq_at(0, 3, False)
+    z_next, z_prev, z_far = (seq_at(0, dz, False) for dz in (1, 3, 2))
     x_next, x_prev, x_far = ({"head": ((x + dx) % 4) * 2 + zl} for dx in (1, 3, 2))
     z_pair = {"head": x * 2 + (1 - zl)}
     line = [
@@ -62,12 +63,11 @@
     w_loads = [pltpu.make_async_copy(w_hbm.at[j], w.at[j], lsem.at[CH + j]) for j in range(3)]
     x_cols = lambda dx: pl.ds(pl.multiple_of(((x + dx) % 4) * 2 * POS, 128), 2 * POS)
     wo_load = pltpu.make_async_copy(wo_hbm.at[:, x_cols(0)], wo.at[0], lsem.at[CH + 3])
-    loads = token_loads + w_loads + [wo_load]
-    for load in loads:
+    for load in token_loads + w_loads[0:1]:
         load.start()
 
     barrier = pltpu.get_barrier_semaphore()
-    peers = [p for p, _ in line] + [z_next, z_prev, x_next, x_prev, x_far, z_pair]
+    peers = [p for p, _ in line] + [z_next, z_prev, z_far, x_next, x_prev, x_far, z_pair]
     for peer in peers:
         pl.semaphore_signal(barrier, inc=1, device_id=peer, device_id_type=MESH)
 
@@ -91,10 +91,8 @@
         for t in range(CH):
             lv[slot, t * RC : (t + 1) * RC, :] = column_of(lrow[slot, t : t + 1, :]).astype(bf16)
 
-    spread_live(0)
-
     def norm_rows(i, carry):
-        rows = pl.ds(pl.multiple_of(i * 16, 16), 16)
+        rows = pl.ds(pl.multiple_of(i * 32, 32), 32)
         v = tok[rows, :].astype(f32)
         center = v - jnp.mean(v, axis=-1, keepdims=True)
         spread = jnp.mean(center * center, axis=-1, keepdims=True)
@@ -103,14 +101,21 @@
 
     for c in range(CH):
         token_loads[c].wait()
-        lax.fori_loop(c * RC // 16, (c + 1) * RC // 16, norm_rows, 0)
+        if c == CH - 1:
+            for load in w_loads[1:] + [wo_load]:
+                load.start()
+        lax.fori_loop(c * RC // 32, (c + 1) * RC // 32, norm_rows, 0)
+
+    score_scale = math.log2(math.e) / math.sqrt(D)
+
+    def project_q(first, last):
+        projected = jnp.dot(normed[...], w[0, :, first * D : last * D], preferred_element_type=f32)
+        for h in range(first, last):
+            gain = qg_ref[h, 0:1, :] * score_scale
+            q[h, 0] = head_norm(projected[:, (h - first) * D : (h - first + 1) * D], gain).astype(bf16)
 
     w_loads[0].wait()
-    projected = jnp.dot(normed[...], w[0], preferred_element_type=f32)
-    score_scale = math.log2(math.e) / math.sqrt(D)
-    for h in range(HEADS):
-        gain = qg_ref[h, 0:1, :] * score_scale
-        q[h, 0] = head_norm(projected[:, h * D : (h + 1) * D], gain).astype(bf16)
+    project_q(0, 1)
 
     pl.semaphore_wait(barrier, len(peers))
 
@@ -121,8 +126,6 @@
         for dx, r, peer in ((1, 1, x_next), (3, 2, x_prev), (2, 3, x_far))
     ]
     wo_sib = [message(wo.at[r, core_rows], wo.at[r, core_rows], sib) for r in (1, 2, 3)]
-    for m in live_msg + wo_msg:
-        m.start()
 
     q_next = [message(q.at[h, 0], q.at[h, 1], z_next) for h in range(HEADS)]
     q_prev = [message(q.at[h, 0], q.at[h, 2], z_prev) for h in range(HEADS)]
@@ -177,7 +180,11 @@
         kv[h, 0, :, D:] = (projected[:, D:] * lv[0].astype(f32)).astype(bf16)
 
     send_q(0)
+    for m in live_msg + wo_msg:
+        m.start()
+    project_q(1, 3)
     send_q(1)
+    spread_live(0)
     w_loads[1].wait()
     w_loads[2].wait()
     project_kv(0)
@@ -205,9 +212,22 @@
             dn[h, c, slot] = acc[slot * RC : (slot + 1) * RC, D:]
 
     A, B = pl.ds(0, HALF), pl.ds(HALF, HALF)
-    zmsg = {}
+    zmsg, dmsg = {}, {}
     for h in range(HEADS):
         for c in range(CH):
+            if (h, c) in DIRECT:
+                i = DIRECT.index((h, c))
+                zmsg[h, c] = [
+                    message(zs.at[h, c, 2], zff.at[i], z_far),
+                    message(zs.at[h, c, 1], zfm.at[h, c], z_next),
+                    message(zs.at[h, c, 0], zfp.at[h, c], z_prev),
+                ]
+                dmsg[h, c] = [
+                    message(ds.at[h, c, 2], dff.at[i], z_far),
+                    message(ds.at[h, c, 1], dfm.at[h, c], z_next),
+                    message(ds.at[h, c, 0], dfp.at[h, c], z_prev),
+                ]
+                continue
             zmsg[h, c] = [
                 message(zs.at[h, c, 2, A], zra.at[h, c], z_next),
                 message(zs.at[h, c, 2, B], zrb.at[h, c], z_prev),
@@ -216,9 +236,6 @@
                 message(zt.at[h, c, 0], zfm.at[h, c, A], z_next),
                 message(zt.at[h, c, 1], zfp.at[h, c, B], z_prev),
             ]
-    dmsg = {}
-    for h in range(HEADS):
-        for c in range(CH):
             dmsg[h, c] = [
                 message(ds.at[h, c, 2], dra.at[h, c], z_next),
                 message(ds.at[h, c, 0], dfp.at[h, c], z_prev),
@@ -233,10 +250,12 @@
         rows = jnp.transpose(mixed)[0:8, :]
         for i in range(3):
             ds[h, c, i] = jnp.broadcast_to(rows[i : i + 1, :], (8, RC))
-        dmsg[h, c][0].start()
-        dmsg[h, c][1].start()
+        for d in dmsg[h, c] if (h, c) in DIRECT else dmsg[h, c][:2]:
+            d.start()
 
     def z_relay(h, c):
+        if (h, c) in DIRECT:
+            return
         m = zmsg[h, c]
         m[0].wait_recv()
         zt[h, c, 0] = (zra[h, c].astype(f32) + zs[h, c, 1, 0:HALF].astype(f32)).astype(bf16)
@@ -253,35 +272,29 @@
     for h in range(HEADS):
         for c in range(CH):
             xmsg[h, c] = [
-                message(xa.at[0, h, c], xa.at[1, h, c], x_next),
-                message(xa.at[0, h, c], xa.at[2, h, c], x_prev),
-                message(xa.at[1, h, c, A], xa.at[3, h, c, A], x_next),
-                message(xa.at[2, h, c, B], xa.at[3, h, c, B], x_prev),
+                message(xa.at[0, h, c], xa.at[r, h, c], peer)
+                for r, peer in ((3, x_far), (1, x_next), (2, x_prev))
             ]
     zlmsg = [message(zls.at[c], zlr.at[c], z_pair) for c in range(CH)]
 
     def attended(h, c):
-        dmsg[h, c][1].wait_recv()
-        dmsg[h, c][2].wait_recv()
-        for m in zmsg[h, c][2:]:
+        direct = (h, c) in DIRECT
+        for m in dmsg[h, c][0 if direct else 1 :] + zmsg[h, c][0 if direct else 2 :]:
             m.wait_recv()
-        den = dn[h, c, 0] + column_of(dfm[h, c, 0:1, :] + dfp[h, c, 0:1, :])
+        others = dfm[h, c, 0:1, :] + dfp[h, c, 0:1, :]
         num = own[h, c] + zfm[h, c].astype(f32) + zfp[h, c].astype(f32)
+        if direct:
+            others = others + dff[DIRECT.index((h, c)), 0:1, :]
+            num = num + zff[DIRECT.index((h, c))].astype(f32)
+        den = dn[h, c, 0] + column_of(others)
         xa[0, h, c] = (num / den).astype(bf16)
-        xmsg[h, c][0].start()
-        xmsg[h, c][1].start()
-
-    def x_forward(h, c):
-        m = xmsg[h, c]
-        m[0].wait_recv()
-        m[2].start()
-        m[1].wait_recv()
-        m[3].start()
+        for m in xmsg[h, c]:
+            m.start()
 
     def project_out(c):
         for h in range(HEADS):
-            xmsg[h, c][2].wait_recv()
-            xmsg[h, c][3].wait_recv()
+            for m in xmsg[h, c]:
+                m.wait_recv()
         rows = jnp.concatenate([xa[r, h, c] for r in range(4) for h in range(HEADS)], axis=1)
         weights = wo[...].reshape(4 * POS, 2 * POS)
         total[c] = jnp.dot(rows, weights, preferred_element_type=f32)
@@ -307,8 +320,6 @@
             z_relay(*steps[u - 2])
         if u >= 4:
             attended(*steps[u - 4])
-        if u >= 5:
-            x_forward(*steps[u - 5])
 
     def step(u):
         unit(*steps[u])
@@ -341,19 +352,14 @@
     z_relay(*steps[7])
     attended(*steps[5])
     z_relay(*steps[8])
-    x_forward(*steps[4])
     wo_load.wait()
     for m in wo_sib:
         m.wait_recv()
     attended(*steps[6])
-    x_forward(*steps[5])
     attended(*steps[7])
-    x_forward(*steps[6])
+    project_out(0)
     attended(*steps[8])
-    project_out(0)
-    x_forward(*steps[7])
     project_out(1)
-    x_forward(*steps[8])
     project_out(2)
     for c in range(CH):
         finish(c)
@@ -361,7 +367,7 @@
         copy.wait_send()
 
 
-MESSAGES = 7 + 6 + 12 + 24 + 54 + 27 + 36 + 3
+MESSAGES = 7 + 6 + 12 + 24 + 54 + 27 - 3 * len(DIRECT) + 27 + 3
 
 
 def per_device(tokens, survive, norm_gain, w_qkv, qk_gain, w_out):
@@ -373,9 +379,9 @@
         vmem(HEADS, 4, POS, D), vmem(HEADS, 8, POS, 2 * D), vmem32(8, 8, 128), vmem(8, POS, D),
         vmem32(*units, RC, D), vmem32(*units, 4, RC, D),
         vmem(*units, 3, RC, D), vmem(*units, HALF, D), vmem(*units, HALF, D),
-        vmem(*units, RC, D), vmem(*units, RC, D), vmem(*units, 2, HALF, D),
+        vmem(*units, RC, D), vmem(*units, RC, D), vmem(len(DIRECT), RC, D), vmem(*units, 2, HALF, D),
         vmem32(*units, 3, 8, RC), vmem32(*units, 8, RC), vmem32(*units, 8, RC), vmem32(*units, 8, RC),
-        vmem32(*units, 8, RC),
+        vmem32(len(DIRECT), 8, RC), vmem32(*units, 8, RC),
         vmem(4, *units, RC, D), vmem32(CH, RC, 2 * POS), vmem(CH, RC, POS), vmem(CH, RC, POS),
         pltpu.SemaphoreType.DMA((CH + 4,)),
         pltpu.SemaphoreType.DMA((MESSAGES,)),

time: 87.7 us -> 80.9 us (0.922)
  Pallas kernels: 85 us -> 78.3 us
    pallas_call x1, Pallas kernels: 85 us -> 78.3 us  [per_device(): pl.pallas_call(kernel, out_shape=jax.ShapeDtypeStruct((POS, POS), bf16),...]
where the time goes in v3:
time: 80.9 us; the launch traced here: 80.8 us
  Pallas kernels  78.3 us (97%)
  other arithmetic  2.49 us (3%)
    pallas_call x1, Pallas kernels, per_device(): pl.pallas_call(kernel, out_shape=jax.ShapeDtypeStruct((POS, POS), bf16),...  78.3 us
    select_n x1, other arithmetic, per_device(): return jnp.where(survive[:, None] == 1, share, jnp.zeros_like(share))  1.8 us

profile of v3, /device:TPU:32, one launch (start us, length us, event | category | flops | bytes accessed | tf_op | source)
XLA Modules:
  0.0 80.8 jit_solution(5342791661425480261)
XLA Ops:
  0.0 0.7 broadcast_compare_fusion
  0.7 78.3 %branch.1 = bf16[384,384]{1,0:T(8,128)(2,1)} custom-call(bf16[384,3072]{1,0:T(8,128)(2,1)} %tok_hbm.1, s32[3,128]{1,0:T(4,128)} %bitcast.6, f32[1,3072]{1,0:T(1,128)} %bitcast.5, bf16[3,3072,384]{2,1,0:T(8,128)(2,1)} %bitcast.4, f32[3,2,128]{2,1,0:T(2,128)} %bitcast.7, bf16[384,3072]{1,0:T(8,128)(2,1)} %wo_hbm.1), custom_call_target="tpu_custom_call" | custom-call | tf_op jit(solution)/shard_map/branch/pallas_call | solution.py:392
  79.0 1.8 %broadcast_select_fusion = bf16[384,384]{1,0:T(8,128)(2,1)} fusion(bf16[384,384]{1,0:T(8,128)(2,1)} %branch.1, pred[384]{0:T(512)(128)(4,1)S(1)} %broadcast_compare_fusion), kind=kLoop, calls=%fused_computation | loop fusion | flops 147456 | bytes 590208 | tf_op jit(solution)/shard_map/jit(_where)/select_n | solution.py:410

commit v4 on v3

--- a/solution.py
+++ b/solution.py
@@ -18,7 +18,7 @@
 CH = 3
 RC = POS // CH
 HALF = RC // 2
-DIRECT = [(2, 2)]
+DIRECT = [(2, 1), (2, 2)]
 
 
 def column_of(row):
@@ -99,25 +99,34 @@
         normed[rows, :] = (center * lax.rsqrt(spread + epsilon) * ng_ref[...]).astype(bf16)
         return carry
 
+    score_scale = math.log2(math.e) / math.sqrt(D)
+    lo, hi = pl.ds(0, POS // 2), pl.ds(POS // 2, POS // 2)
+    q_next, q_prev, q_fwd_next, q_fwd_prev = [], [], [], []
+    for c in range(CH):
+        rows = pl.ds(c * RC, RC)
+        first, second = pl.ds(c * RC, HALF), pl.ds(c * RC + HALF, HALF)
+        q_next.append(message(q.at[0, :, rows], q.at[1, :, rows], z_next))
+        q_prev.append(message(q.at[0, :, rows], q.at[2, :, rows], z_prev))
+        q_fwd_next.append(message(q.at[1, :, first], q.at[3, :, first], z_next))
+        q_fwd_prev.append(message(q.at[2, :, second], q.at[3, :, second], z_prev))
+
     for c in range(CH):
         token_loads[c].wait()
         if c == CH - 1:
             for load in w_loads[1:] + [wo_load]:
                 load.start()
         lax.fori_loop(c * RC // 32, (c + 1) * RC // 32, norm_rows, 0)
-
-    score_scale = math.log2(math.e) / math.sqrt(D)
-
-    def project_q(first, last):
-        projected = jnp.dot(normed[...], w[0, :, first * D : last * D], preferred_element_type=f32)
-        for h in range(first, last):
+        if c == 0:
+            w_loads[0].wait()
+        rows = slice(c * RC, (c + 1) * RC)
+        projected = jnp.dot(normed[rows, :], w[0], preferred_element_type=f32)
+        for h in range(HEADS):
             gain = qg_ref[h, 0:1, :] * score_scale
-            q[h, 0] = head_norm(projected[:, (h - first) * D : (h - first + 1) * D], gain).astype(bf16)
-
-    w_loads[0].wait()
-    project_q(0, 1)
-
-    pl.semaphore_wait(barrier, len(peers))
+            q[0, h, rows, :] = head_norm(projected[:, h * D : (h + 1) * D], gain).astype(bf16)
+        if c == 0:
+            pl.semaphore_wait(barrier, len(peers))
+        q_next[c].start()
+        q_prev[c].start()
 
     live_msg = [message(lrow.at[0], lrow.at[slot], peer) for peer, slot in line]
     core_rows = pl.ds(pl.multiple_of(co * (POS // 2), 16), POS // 2)
@@ -127,38 +136,32 @@
     ]
     wo_sib = [message(wo.at[r, core_rows], wo.at[r, core_rows], sib) for r in (1, 2, 3)]
 
-    q_next = [message(q.at[h, 0], q.at[h, 1], z_next) for h in range(HEADS)]
-    q_prev = [message(q.at[h, 0], q.at[h, 2], z_prev) for h in range(HEADS)]
-    lo, hi = pl.ds(0, POS // 2), pl.ds(POS // 2, POS // 2)
-    q_fwd_next = [message(q.at[h, 1, lo], q.at[h, 3, lo], z_next) for h in range(HEADS)]
-    q_fwd_prev = [message(q.at[h, 2, hi], q.at[h, 3, hi], z_prev) for h in range(HEADS)]
-    kv_next = [message(kv.at[h, 0], kv.at[h, 2], y_next) for h in range(HEADS)]
-    kv_prev = [message(kv.at[h, 0], kv.at[h, 4], y_prev) for h in range(HEADS)]
+    kv_next = [[message(kv.at[h, 0, half], kv.at[h, 2, half], y_next) for half in (lo, hi)] for h in range(HEADS)]
+    kv_prev = [[message(kv.at[h, 0, half], kv.at[h, 4, half], y_prev) for half in (hi, lo)] for h in range(HEADS)]
     kv_fwd_next = [message(kv.at[h, 2, lo], kv.at[h, 6, lo], y_next) for h in range(HEADS)]
     kv_fwd_prev = [message(kv.at[h, 4, hi], kv.at[h, 6, hi], y_prev) for h in range(HEADS)]
     kv_sib = [[message(kv.at[h, 2 * r], kv.at[h, 2 * r + 1], sib) for r in range(4)] for h in range(HEADS)]
 
-    def send_q(h):
-        q_next[h].start()
-        q_prev[h].start()
-
-    def send_kv(h):
-        kv_next[h].start()
-        kv_prev[h].start()
-        kv_sib[h][0].start()
-
-    def forward_q(h):
-        q_next[h].wait_recv()
-        q_fwd_next[h].start()
-        q_prev[h].wait_recv()
-        q_fwd_prev[h].start()
+    def send_kv(h, part):
+        kv_next[h][part].start()
+        kv_prev[h][part].start()
+
+    def forward_q(c):
+        q_next[c].wait_recv()
+        q_fwd_next[c].start()
+        q_prev[c].wait_recv()
+        q_fwd_prev[c].start()
 
     def forward_kv(h):
-        kv_next[h].wait_recv()
+        kv_next[h][0].wait_recv()
         kv_fwd_next[h].start()
+        kv_prev[h][0].wait_recv()
+        kv_fwd_prev[h].start()
+
+    def share_near(h):
+        kv_next[h][1].wait_recv()
         kv_sib[h][1].start()
-        kv_prev[h].wait_recv()
-        kv_fwd_prev[h].start()
+        kv_prev[h][1].wait_recv()
         kv_sib[h][2].start()
 
     def share_far(h):
@@ -166,9 +169,11 @@
         kv_fwd_prev[h].wait_recv()
         kv_sib[h][3].start()
 
+    def queries_in(c):
+        q_fwd_next[c].wait_recv()
+        q_fwd_prev[c].wait_recv()
+
     def all_in(h):
-        q_fwd_next[h].wait_recv()
-        q_fwd_prev[h].wait_recv()
         for m in kv_sib[h]:
             m.wait_recv()
 
@@ -179,27 +184,34 @@
         kv[h, 0, :, 0:D] = head_norm(projected[:, :D], qg_ref[h, 1:2, :]).astype(bf16)
         kv[h, 0, :, D:] = (projected[:, D:] * lv[0].astype(f32)).astype(bf16)
 
-    send_q(0)
     for m in live_msg + wo_msg:
         m.start()
-    project_q(1, 3)
-    send_q(1)
     spread_live(0)
     w_loads[1].wait()
     w_loads[2].wait()
     project_kv(0)
-    send_kv(0)
+    send_kv(0, 0)
+    send_kv(0, 1)
+    kv_sib[0][0].start()
     project_kv(1)
-    send_kv(1)
+    send_kv(1, 0)
+    kv_sib[1][0].start()
+    forward_q(0)
     project_kv(2)
-
-    for m, (_, slot) in zip(live_msg, line):
+    kv_sib[2][0].start()
+    for m, (_, slot) in zip(live_msg[:3], line[:3]):
         m.wait_recv()
         spread_live(slot)
+    forward_kv(0)
+    send_kv(1, 1)
+    send_kv(2, 0)
+    for m, (_, slot) in zip(live_msg[3:], line[3:]):
+        m.wait_recv()
+        spread_live(slot)
 
     def unit(h, c):
         rows = pl.ds(c * RC, RC)
-        queries = jnp.concatenate([q[h, slot, rows, :] for slot in range(4)], axis=0)
+        queries = jnp.concatenate([q[slot, h, rows, :] for slot in range(4)], axis=0)
         keys = kv[h, :, :, 0:D].reshape(8 * POS, D)
         scores = lax.dot_general(queries, keys, (((1,), (1,)), ((), ())), preferred_element_type=f32)
         weights = jnp.exp2(scores).astype(bf16)
@@ -249,7 +261,7 @@
         mixed = jnp.where(lane == 0, dn[h, c, 1], jnp.where(lane == 1, dn[h, c, 2], dn[h, c, 3]))
         rows = jnp.transpose(mixed)[0:8, :]
         for i in range(3):
-            ds[h, c, i] = jnp.broadcast_to(rows[i : i + 1, :], (8, RC))
+            ds[h, c, i] = rows[i : i + 1, :]
         for d in dmsg[h, c] if (h, c) in DIRECT else dmsg[h, c][:2]:
             d.start()
 
@@ -281,10 +293,10 @@
         direct = (h, c) in DIRECT
         for m in dmsg[h, c][0 if direct else 1 :] + zmsg[h, c][0 if direct else 2 :]:
             m.wait_recv()
-        others = dfm[h, c, 0:1, :] + dfp[h, c, 0:1, :]
+        others = dfm[h, c] + dfp[h, c]
         num = own[h, c] + zfm[h, c].astype(f32) + zfp[h, c].astype(f32)
         if direct:
-            others = others + dff[DIRECT.index((h, c)), 0:1, :]
+            others = others + dff[DIRECT.index((h, c))]
             num = num + zff[DIRECT.index((h, c))].astype(f32)
         den = dn[h, c, 0] + column_of(others)
         xa[0, h, c] = (num / den).astype(bf16)
@@ -296,16 +308,16 @@
             for m in xmsg[h, c]:
                 m.wait_recv()
         rows = jnp.concatenate([xa[r, h, c] for r in range(4) for h in range(HEADS)], axis=1)
-        weights = wo[...].reshape(4 * POS, 2 * POS)
-        total[c] = jnp.dot(rows, weights, preferred_element_type=f32)
         other = pl.ds(pl.multiple_of((1 - zl) * POS, 128), POS)
-        zls[c] = total[c, :, other].astype(bf16)
+        mine = pl.ds(pl.multiple_of(zl * POS, 128), POS)
+        theirs = wo[:, :, other].reshape(4 * POS, POS)
+        zls[c] = jnp.dot(rows, theirs, preferred_element_type=f32).astype(bf16)
         zlmsg[c].start()
+        total[c] = jnp.dot(rows, wo[:, :, mine].reshape(4 * POS, POS), preferred_element_type=f32)
 
     def finish(c):
         zlmsg[c].wait_recv()
-        mine = pl.ds(pl.multiple_of(zl * POS, 128), POS)
-        out_ref[c * RC : (c + 1) * RC, :] = (total[c, :, mine] + zlr[c].astype(f32)).astype(bf16)
+        out_ref[c * RC : (c + 1) * RC, :] = (total[c] + zlr[c].astype(f32)).astype(bf16)
 
     def share_weights():
         for m, share in zip(wo_msg, wo_sib):
@@ -325,23 +337,26 @@
         unit(*steps[u])
         after(u)
 
-    forward_q(0)
-    forward_kv(0)
-    send_q(2)
-    send_kv(2)
+    share_near(0)
     forward_q(1)
     forward_kv(1)
+    send_kv(2, 1)
     share_far(0)
+    queries_in(0)
     all_in(0)
     step(0)
     forward_q(2)
+    share_near(1)
     forward_kv(2)
+    queries_in(1)
     step(1)
     share_far(1)
+    share_near(2)
+    queries_in(2)
     step(2)
     all_in(1)
+    share_far(2)
     step(3)
-    share_far(2)
     step(4)
     share_weights()
     step(5)
@@ -349,9 +364,7 @@
     step(6)
     step(7)
     step(8)
-    z_relay(*steps[7])
     attended(*steps[5])
-    z_relay(*steps[8])
     wo_load.wait()
     for m in wo_sib:
         m.wait_recv()
@@ -367,7 +380,7 @@
         copy.wait_send()
 
 
-MESSAGES = 7 + 6 + 12 + 24 + 54 + 27 - 3 * len(DIRECT) + 27 + 3
+MESSAGES = 7 + 6 + 12 + 30 + 54 + 27 - 3 * len(DIRECT) + 27 + 3
 
 
 def per_device(tokens, survive, norm_gain, w_qkv, qk_gain, w_out):
@@ -376,13 +389,13 @@
     units = (HEADS, CH)
     scratch = [
         vmem(POS, WIDTH), vmem(POS, WIDTH), vmem(3, WIDTH, POS), vmem(4, POS, 2 * POS),
-        vmem(HEADS, 4, POS, D), vmem(HEADS, 8, POS, 2 * D), vmem32(8, 8, 128), vmem(8, POS, D),
+        vmem(4, HEADS, POS, D), vmem(HEADS, 8, POS, 2 * D), vmem32(8, 8, 128), vmem(8, POS, D),
         vmem32(*units, RC, D), vmem32(*units, 4, RC, D),
         vmem(*units, 3, RC, D), vmem(*units, HALF, D), vmem(*units, HALF, D),
         vmem(*units, RC, D), vmem(*units, RC, D), vmem(len(DIRECT), RC, D), vmem(*units, 2, HALF, D),
-        vmem32(*units, 3, 8, RC), vmem32(*units, 8, RC), vmem32(*units, 8, RC), vmem32(*units, 8, RC),
-        vmem32(len(DIRECT), 8, RC), vmem32(*units, 8, RC),
-        vmem(4, *units, RC, D), vmem32(CH, RC, 2 * POS), vmem(CH, RC, POS), vmem(CH, RC, POS),
+        vmem32(*units, 3, 1, RC), vmem32(*units, 1, RC), vmem32(*units, 1, RC), vmem32(*units, 1, RC),
+        vmem32(len(DIRECT), 1, RC), vmem32(*units, 1, RC),
+        vmem(4, *units, RC, D), vmem32(CH, RC, POS), vmem(CH, RC, POS), vmem(CH, RC, POS),
         pltpu.SemaphoreType.DMA((CH + 4,)),
         pltpu.SemaphoreType.DMA((MESSAGES,)),
         pltpu.SemaphoreType.DMA((MESSAGES,)),

time: 80.9 us -> 81.9 us (1.012)
  Pallas kernels: 78.3 us -> 79.2 us
    pallas_call x1, Pallas kernels: 78.3 us -> 79.2 us  [per_device(): pl.pallas_call(kernel, out_shape=jax.ShapeDtypeStruct((POS, POS), bf16),...]
where the time goes in v4:
time: 81.9 us; the launch traced here: 81.7 us
  Pallas kernels  79.2 us (97%)
  other arithmetic  2.49 us (3%)
    pallas_call x1, Pallas kernels, per_device(): pl.pallas_call(kernel, out_shape=jax.ShapeDtypeStruct((POS, POS), bf16),...  79.2 us
    select_n x1, other arithmetic, per_device(): return jnp.where(survive[:, None] == 1, share, jnp.zeros_like(share))  1.8 us

profile of v4, /device:TPU:32, one launch (start us, length us, event | category | flops | bytes accessed | tf_op | source)
XLA Modules:
  0.0 81.7 jit_solution(7159595266528184958)
XLA Ops:
  0.0 0.7 broadcast_compare_fusion
  0.7 79.2 %branch.1 = bf16[384,384]{1,0:T(8,128)(2,1)} custom-call(bf16[384,3072]{1,0:T(8,128)(2,1)} %tok_hbm.1, s32[3,128]{1,0:T(4,128)} %bitcast.6, f32[1,3072]{1,0:T(1,128)} %bitcast.5, bf16[3,3072,384]{2,1,0:T(8,128)(2,1)} %bitcast.4, f32[3,2,128]{2,1,0:T(2,128)} %bitcast.7, bf16[384,3072]{1,0:T(8,128)(2,1)} %wo_hbm.1), custom_call_target="tpu_custom_call" | custom-call | tf_op jit(solution)/shard_map/branch/pallas_call | solution.py:405
  79.9 1.8 %broadcast_select_fusion = bf16[384,384]{1,0:T(8,128)(2,1)} fusion(bf16[384,384]{1,0:T(8,128)(2,1)} %branch.1, pred[384]{0:T(512)(128)(4,1)S(1)} %broadcast_compare_fusion), kind=kLoop, calls=%fused_computation | loop fusion | flops 147456 | bytes 590208 | tf_op jit(solution)/shard_map/jit(_where)/select_n | solution.py:423

commit v5 on v4

--- a/solution.py
+++ b/solution.py
@@ -18,7 +18,7 @@
 CH = 3
 RC = POS // CH
 HALF = RC // 2
-DIRECT = [(2, 1), (2, 2)]
+DIRECT = [(2, 0), (2, 1), (2, 2)]
 
 
 def column_of(row):
@@ -125,8 +125,9 @@
             q[0, h, rows, :] = head_norm(projected[:, h * D : (h + 1) * D], gain).astype(bf16)
         if c == 0:
             pl.semaphore_wait(barrier, len(peers))
-        q_next[c].start()
-        q_prev[c].start()
+        if c < CH - 1:
+            q_next[c].start()
+            q_prev[c].start()
 
     live_msg = [message(lrow.at[0], lrow.at[slot], peer) for peer, slot in line]
     core_rows = pl.ds(pl.multiple_of(co * (POS // 2), 16), POS // 2)
@@ -197,6 +198,8 @@
     send_kv(1, 0)
     kv_sib[1][0].start()
     forward_q(0)
+    q_next[2].start()
+    q_prev[2].start()
     project_kv(2)
     kv_sib[2][0].start()
     for m, (_, slot) in zip(live_msg[:3], line[:3]):
@@ -330,8 +333,6 @@
         z_first(*steps[u])
         if u >= 2:
             z_relay(*steps[u - 2])
-        if u >= 4:
-            attended(*steps[u - 4])
 
     def step(u):
         unit(*steps[u])
@@ -364,7 +365,8 @@
     step(6)
     step(7)
     step(8)
-    attended(*steps[5])
+    for u in range(6):
+        attended(*steps[u])
     wo_load.wait()
     for m in wo_sib:
         m.wait_recv()

time: 81.9 us -> 80.8 us (0.987); the launches traced: 81.7 us -> 79.7 us
  Pallas kernels: 79.2 us -> 77.2 us
    pallas_call x1, Pallas kernels: 79.2 us -> 77.2 us  [per_device(): pl.pallas_call(kernel, out_shape=jax.ShapeDtypeStruct((POS, POS), bf16),...]
where the time goes in v5:
time: 80.8 us; the launch traced here: 79.7 us
  Pallas kernels  77.2 us (96%)
  other arithmetic  2.49 us (3%)
    pallas_call x1, Pallas kernels, per_device(): pl.pallas_call(kernel, out_shape=jax.ShapeDtypeStruct((POS, POS), bf16),...  77.2 us
    select_n x1, other arithmetic, per_device(): return jnp.where(survive[:, None] == 1, share, jnp.zeros_like(share))  1.8 us

profile of v5, /device:TPU:32, one launch (start us, length us, event | category | flops | bytes accessed | tf_op | source)
XLA Modules:
  0.0 79.7 jit_solution(11563114724134100711)
XLA Ops:
  0.0 0.7 broadcast_compare_fusion
  0.7 77.2 %branch.1 = bf16[384,384]{1,0:T(8,128)(2,1)} custom-call(bf16[384,3072]{1,0:T(8,128)(2,1)} %tok_hbm.1, s32[3,128]{1,0:T(4,128)} %bitcast.6, f32[1,3072]{1,0:T(1,128)} %bitcast.5, bf16[3,3072,384]{2,1,0:T(8,128)(2,1)} %bitcast.4, f32[3,2,128]{2,1,0:T(2,128)} %bitcast.7, bf16[384,3072]{1,0:T(8,128)(2,1)} %wo_hbm.1), custom_call_target="tpu_custom_call" | custom-call | tf_op jit(solution)/shard_map/branch/pallas_call | solution.py:407
  77.9 1.8 %broadcast_select_fusion = bf16[384,384]{1,0:T(8,128)(2,1)} fusion(bf16[384,384]{1,0:T(8,128)(2,1)} %branch.1, pred[384]{0:T(512)(128)(4,1)S(1)} %broadcast_compare_fusion), kind=kLoop, calls=%fused_computation | loop fusion | flops 147456 | bytes 590208 | tf_op jit(solution)/shard_map/jit(_where)/select_n | solution.py:425

commit v6 on v5

--- a/solution.py
+++ b/solution.py
@@ -110,24 +110,28 @@
         q_fwd_next.append(message(q.at[1, :, first], q.at[3, :, first], z_next))
         q_fwd_prev.append(message(q.at[2, :, second], q.at[3, :, second], z_prev))
 
+    def project_q(c):
+        rows = slice(c * RC, (c + 1) * RC)
+        projected = jnp.dot(normed[rows, :], w[0], preferred_element_type=f32)
+        for h in range(HEADS):
+            gain = qg_ref[h, 0:1, :] * score_scale
+            q[0, h, rows, :] = head_norm(projected[:, h * D : (h + 1) * D], gain).astype(bf16)
+
+    def send_q(c):
+        q_next[c].start()
+        q_prev[c].start()
+
     for c in range(CH):
         token_loads[c].wait()
-        if c == CH - 1:
+        if c == 1:
             for load in w_loads[1:] + [wo_load]:
                 load.start()
         lax.fori_loop(c * RC // 32, (c + 1) * RC // 32, norm_rows, 0)
         if c == 0:
             w_loads[0].wait()
-        rows = slice(c * RC, (c + 1) * RC)
-        projected = jnp.dot(normed[rows, :], w[0], preferred_element_type=f32)
-        for h in range(HEADS):
-            gain = qg_ref[h, 0:1, :] * score_scale
-            q[0, h, rows, :] = head_norm(projected[:, h * D : (h + 1) * D], gain).astype(bf16)
-        if c == 0:
+            project_q(0)
             pl.semaphore_wait(barrier, len(peers))
-        if c < CH - 1:
-            q_next[c].start()
-            q_prev[c].start()
+            send_q(0)
 
     live_msg = [message(lrow.at[0], lrow.at[slot], peer) for peer, slot in line]
     core_rows = pl.ds(pl.multiple_of(co * (POS // 2), 16), POS // 2)
@@ -194,12 +198,14 @@
     send_kv(0, 0)
     send_kv(0, 1)
     kv_sib[0][0].start()
+    project_q(1)
+    send_q(1)
+    project_q(2)
     project_kv(1)
     send_kv(1, 0)
     kv_sib[1][0].start()
     forward_q(0)
-    q_next[2].start()
-    q_prev[2].start()
+    send_q(2)
     project_kv(2)
     kv_sib[2][0].start()
     for m, (_, slot) in zip(live_msg[:3], line[:3]):
@@ -212,19 +218,29 @@
         m.wait_recv()
         spread_live(slot)
 
-    def unit(h, c):
-        rows = pl.ds(c * RC, RC)
-        queries = jnp.concatenate([q[slot, h, rows, :] for slot in range(4)], axis=0)
+    def attend(queries, h):
         keys = kv[h, :, :, 0:D].reshape(8 * POS, D)
         scores = lax.dot_general(queries, keys, (((1,), (1,)), ((), ())), preferred_element_type=f32)
         weights = jnp.exp2(scores).astype(bf16)
         values = jnp.concatenate([kv[h, :, :, D:].reshape(8 * POS, D), lv[...].reshape(8 * POS, D)], axis=1)
-        acc = jnp.dot(weights, values, preferred_element_type=f32)
-        own[h, c] = acc[0:RC, 0:D]
-        for slot in range(1, 4):
-            zs[h, c, slot - 1] = acc[slot * RC : (slot + 1) * RC, 0:D].astype(bf16)
-        for slot in range(4):
-            dn[h, c, slot] = acc[slot * RC : (slot + 1) * RC, D:]
+        return jnp.dot(weights, values, preferred_element_type=f32)
+
+    def keep(acc, h, c, slot):
+        if slot == 0:
+            own[h, c] = acc[:, 0:D]
+        else:
+            zs[h, c, slot - 1] = acc[:, 0:D].astype(bf16)
+        dn[h, c, slot] = acc[:, D:]
+
+    def unit(h, c, slots):
+        acc = attend(jnp.concatenate([q[slot, h, c * RC : (c + 1) * RC, :] for slot in slots], axis=0), h)
+        for i, slot in enumerate(slots):
+            keep(acc[i * RC : (i + 1) * RC], h, c, slot)
+
+    def far_unit(h):
+        acc = attend(q[3, h], h)
+        for c in range(CH):
+            keep(acc[c * RC : (c + 1) * RC], h, c, 3)
 
     A, B = pl.ds(0, HALF), pl.ds(HALF, HALF)
     zmsg, dmsg = {}, {}
@@ -257,8 +273,12 @@
                 message(dt.at[h, c], dfm.at[h, c], z_next),
             ]
 
-    def z_first(h, c):
-        for m in zmsg[h, c][:4]:
+    def z_near(h, c):
+        for m in zmsg[h, c][2:4]:
+            m.start()
+
+    def z_first(h, c, sends):
+        for m in zmsg[h, c][sends]:
             m.start()
         lane = lax.broadcasted_iota(jnp.int32, (RC, D), 1)
         mixed = jnp.where(lane == 0, dn[h, c, 1], jnp.where(lane == 1, dn[h, c, 2], dn[h, c, 3]))
@@ -320,7 +340,9 @@
 
     def finish(c):
         zlmsg[c].wait_recv()
-        out_ref[c * RC : (c + 1) * RC, :] = (total[c] + zlr[c].astype(f32)).astype(bf16)
+        mask = jnp.concatenate([lv[0, c * RC : (c + 1) * RC, :].astype(f32)] * (POS // D), axis=1)
+        share = jnp.where(mask > 0.5, total[c] + zlr[c].astype(f32), 0.0)
+        out_ref[c * RC : (c + 1) * RC, :] = share.astype(bf16)
 
     def share_weights():
         for m, share in zip(wo_msg, wo_sib):
@@ -329,41 +351,47 @@
 
     steps = [(h, c) for h in range(HEADS) for c in range(CH)]
 
-    def after(u):
-        z_first(*steps[u])
-        if u >= 2:
-            z_relay(*steps[u - 2])
-
     def step(u):
-        unit(*steps[u])
-        after(u)
+        unit(*steps[u], range(4))
+        z_first(*steps[u], slice(0, 4))
 
     share_near(0)
     forward_q(1)
     forward_kv(1)
     send_kv(2, 1)
     share_far(0)
-    queries_in(0)
     all_in(0)
-    step(0)
+    unit(0, 0, range(3))
+    z_near(0, 0)
     forward_q(2)
     share_near(1)
     forward_kv(2)
-    queries_in(1)
-    step(1)
+    unit(0, 1, range(3))
+    z_near(0, 1)
     share_far(1)
+    unit(0, 2, range(3))
+    z_near(0, 2)
     share_near(2)
-    queries_in(2)
-    step(2)
+    for c in range(CH):
+        queries_in(c)
+    far_unit(0)
+    for c in range(CH):
+        z_first(0, c, slice(0, 2))
     all_in(1)
+    step(3)
     share_far(2)
-    step(3)
     step(4)
+    z_relay(0, 0)
+    z_relay(0, 1)
     share_weights()
     step(5)
+    z_relay(0, 2)
+    z_relay(1, 0)
     all_in(2)
     step(6)
+    z_relay(1, 1)
     step(7)
+    z_relay(1, 2)
     step(8)
     for u in range(6):
         attended(*steps[u])
@@ -404,7 +432,7 @@
     ]
     in_hbm = pl.BlockSpec(memory_space=pl.ANY)
     in_vmem = pl.BlockSpec(memory_space=pltpu.VMEM)
-    share = pl.pallas_call(
+    return pl.pallas_call(
         kernel,
         out_shape=jax.ShapeDtypeStruct((POS, POS), bf16),
         in_specs=[in_hbm, in_vmem, in_vmem, in_hbm, in_vmem, in_hbm],
@@ -422,7 +450,6 @@
         jnp.transpose(qk_gain, (1, 0, 2)),
         w_out,
     )
-    return jnp.where(survive[:, None] == 1, share, jnp.zeros_like(share))
 
 
 def solution(mesh):

time: 80.8 us -> 78.1 us (0.967)
  other arithmetic: 2.49 us -> 0 us
  Pallas kernels: 77.2 us -> 74.9 us
  local copies, waits for them, and re-layouts: 0 us -> 1.71 us
    pallas_call x1, Pallas kernels: 77.2 us -> 74.9 us  [per_device(): pl.pallas_call(kernel, out_shape=jax.ShapeDtypeStruct((POS, POS), bf16),...]
    select_n x1 -> x0, other arithmetic: 1.8 us -> none  [per_device(): return jnp.where(survive[:, None] == 1, share, jnp.zeros_like(share))]
    unnamed x0 -> x1, local copies, waits for them, and re-layouts: none -> 1.71 us
where the time goes in v6:
time: 78.1 us; the launch traced here: 76.6 us
  Pallas kernels  74.9 us (96%)
  local copies, waits for them, and re-layouts  1.71 us (2%)
    pallas_call x1, Pallas kernels, per_device(): pl.pallas_call(kernel, out_shape=jax.ShapeDtypeStruct((POS, POS), bf16),...  74.9 us
    unnamed x1, local copies, waits for them, and re-layouts  1.71 us

profile of v6, /device:TPU:32, one launch (start us, length us, event | category | flops | bytes accessed | tf_op | source)
XLA Modules:
  0.0 76.6 jit_solution(7795305263655087786)
XLA Ops:
  0.0 74.9 %branch.1 = bf16[384,384]{1,0:T(8,128)(2,1)} custom-call(bf16[384,3072]{1,0:T(8,128)(2,1)} %tok_hbm.1, s32[3,128]{1,0:T(4,128)} %bitcast.7, f32[1,3072]{1,0:T(1,128)} %bitcast.5, bf16[3,3072,384]{2,1,0:T(8,128)(2,1)} %bitcast.4, f32[3,2,128]{2,1,0:T(2,128)} %bitcast.6, bf16[384,3072]{1,0:T(8,128)(2,1)} %wo_hbm.1), custom_call_target="tpu_custom_call" | custom-call | tf_op jit(solution)/shard_map/branch/pallas_call | solution.py:435
  74.9 1.7 %copy.8 = bf16[384,384]{1,0:T(8,128)(2,1)} copy(bf16[384,384]{1,0:T(8,128)(2,1)} %branch.1) | data formatting | bytes 589824

commit v7 on v6

--- a/solution.py
+++ b/solution.py
@@ -18,7 +18,8 @@
 CH = 3
 RC = POS // CH
 HALF = RC // 2
-DIRECT = [(2, 0), (2, 1), (2, 2)]
+LAST = HEADS - 1
+PIECES = [(0, 0, RC), (1, 0, RC), (2, 0, RC)]
 
 
 def column_of(row):
@@ -32,10 +33,11 @@
 
 
 def kernel(
-    tok_hbm, sv_ref, ng_ref, w_hbm, qg_ref, wo_hbm, out_ref,
+    tok_hbm, sv_hbm, ng_hbm, w_hbm, qg_hbm, wo_hbm, out_ref,
+    sv_ref, ng_ref, qg_ref,
     tok, normed, w, wo, q, kv, lrow, lv, own, dn,
-    zs, zra, zrb, zfm, zfp, zff, zt, ds, dra, dfm, dfp, dff, dt,
-    xa, total, zls, zlr,
+    zs, zra, zrb, zfm, zfp, zff, zt, ds, dra, dfm, dfp, dt, dps, dpf,
+    xa, total, given, zls, zlr,
     lsem, ssem, rsem,
 ):
     s = lax.axis_index("seq")
@@ -63,7 +65,11 @@
     w_loads = [pltpu.make_async_copy(w_hbm.at[j], w.at[j], lsem.at[CH + j]) for j in range(3)]
     x_cols = lambda dx: pl.ds(pl.multiple_of(((x + dx) % 4) * 2 * POS, 128), 2 * POS)
     wo_load = pltpu.make_async_copy(wo_hbm.at[:, x_cols(0)], wo.at[0], lsem.at[CH + 3])
-    for load in token_loads + w_loads[0:1]:
+    small_loads = [
+        pltpu.make_async_copy(src, dst, lsem.at[CH + 4 + i])
+        for i, (src, dst) in enumerate(((ng_hbm, ng_ref), (sv_hbm, sv_ref), (qg_hbm, qg_ref)))
+    ]
+    for load in token_loads[0:1] + small_loads + token_loads[1:] + w_loads[0:1]:
         load.start()
 
     barrier = pltpu.get_barrier_semaphore()
@@ -84,8 +90,6 @@
         sent.append(copy)
         return copy
 
-    lrow[0] = jnp.zeros((8, 128), f32)
-    lrow[0, 0:CH, :] = (sv_ref[...] == 1).astype(f32)
 
     def spread_live(slot):
         for t in range(CH):
@@ -121,6 +125,10 @@
         q_next[c].start()
         q_prev[c].start()
 
+    for load in small_loads:
+        load.wait()
+    lrow[0] = jnp.zeros((8, 128), f32)
+    lrow[0, 0:CH, :] = (sv_ref[...] == 1).astype(f32)
     for c in range(CH):
         token_loads[c].wait()
         if c == 1:
@@ -244,21 +252,8 @@
 
     A, B = pl.ds(0, HALF), pl.ds(HALF, HALF)
     zmsg, dmsg = {}, {}
-    for h in range(HEADS):
+    for h in range(LAST):
         for c in range(CH):
-            if (h, c) in DIRECT:
-                i = DIRECT.index((h, c))
-                zmsg[h, c] = [
-                    message(zs.at[h, c, 2], zff.at[i], z_far),
-                    message(zs.at[h, c, 1], zfm.at[h, c], z_next),
-                    message(zs.at[h, c, 0], zfp.at[h, c], z_prev),
-                ]
-                dmsg[h, c] = [
-                    message(ds.at[h, c, 2], dff.at[i], z_far),
-                    message(ds.at[h, c, 1], dfm.at[h, c], z_next),
-                    message(ds.at[h, c, 0], dfp.at[h, c], z_prev),
-                ]
-                continue
             zmsg[h, c] = [
                 message(zs.at[h, c, 2, A], zra.at[h, c], z_next),
                 message(zs.at[h, c, 2, B], zrb.at[h, c], z_prev),
@@ -273,6 +268,29 @@
                 message(dt.at[h, c], dfm.at[h, c], z_next),
             ]
 
+    def part(p):
+        c, row, n = PIECES[p]
+        return c, pl.ds(row, n)
+
+    for p in range(len(PIECES)):
+        c, rows = part(p)
+        zmsg[p] = [
+            message(zs.at[LAST, c, 2, rows], zff.at[c, rows], z_far),
+            message(zs.at[LAST, c, 1, rows], zfm.at[LAST, c, rows], z_next),
+            message(zs.at[LAST, c, 0, rows], zfp.at[LAST, c, rows], z_prev),
+        ]
+        dmsg[p] = [
+            message(dps.at[p, 2], dpf.at[p, 2], z_far),
+            message(dps.at[p, 1], dpf.at[p, 1], z_next),
+            message(dps.at[p, 0], dpf.at[p, 0], z_prev),
+        ]
+
+    def den_rows(d1, d2, d3):
+        lane = lax.broadcasted_iota(jnp.int32, d1.shape, 1)
+        mixed = jnp.where(lane == 0, d1, jnp.where(lane == 1, d2, d3))
+        mixed = jnp.concatenate([mixed] * (RC // d1.shape[0]), axis=0)
+        return jnp.transpose(mixed)[0:8, :]
+
     def z_near(h, c):
         for m in zmsg[h, c][2:4]:
             m.start()
@@ -280,17 +298,30 @@
     def z_first(h, c, sends):
         for m in zmsg[h, c][sends]:
             m.start()
-        lane = lax.broadcasted_iota(jnp.int32, (RC, D), 1)
-        mixed = jnp.where(lane == 0, dn[h, c, 1], jnp.where(lane == 1, dn[h, c, 2], dn[h, c, 3]))
-        rows = jnp.transpose(mixed)[0:8, :]
+        rows = den_rows(dn[h, c, 1], dn[h, c, 2], dn[h, c, 3])
         for i in range(3):
             ds[h, c, i] = rows[i : i + 1, :]
-        for d in dmsg[h, c] if (h, c) in DIRECT else dmsg[h, c][:2]:
+        for d in dmsg[h, c][:2]:
             d.start()
 
+    def last_step(p):
+        c, rows = part(p)
+        n = PIECES[p][2]
+        first = c * RC + PIECES[p][1]
+        acc = attend(jnp.concatenate([q[slot, LAST, first : first + n, :] for slot in range(4)], axis=0), LAST)
+        own[LAST, c, rows] = acc[0:n, 0:D]
+        dn[LAST, c, 0, rows] = acc[0:n, D:]
+        for slot in range(1, 4):
+            zs[LAST, c, slot - 1, rows] = acc[slot * n : (slot + 1) * n, 0:D].astype(bf16)
+        for m in zmsg[p]:
+            m.start()
+        dens = den_rows(*(acc[slot * n : (slot + 1) * n, D:] for slot in range(1, 4)))
+        for i in range(3):
+            dps[p, i] = dens[i : i + 1, :]
+        for d in dmsg[p]:
+            d.start()
+
     def z_relay(h, c):
-        if (h, c) in DIRECT:
-            return
         m = zmsg[h, c]
         m[0].wait_recv()
         zt[h, c, 0] = (zra[h, c].astype(f32) + zs[h, c, 1, 0:HALF].astype(f32)).astype(bf16)
@@ -304,56 +335,87 @@
         d[2].start()
 
     xmsg = {}
-    for h in range(HEADS):
+    for h in range(LAST):
         for c in range(CH):
             xmsg[h, c] = [
                 message(xa.at[0, h, c], xa.at[r, h, c], peer)
                 for r, peer in ((3, x_far), (1, x_next), (2, x_prev))
             ]
-    zlmsg = [message(zls.at[c], zlr.at[c], z_pair) for c in range(CH)]
+    zlmsg = []
+    for p in range(len(PIECES)):
+        c, rows = part(p)
+        xmsg[p] = [
+            message(xa.at[0, LAST, c, rows], xa.at[r, LAST, c, rows], peer)
+            for r, peer in ((3, x_far), (1, x_next), (2, x_prev))
+        ]
+        zlmsg.append(message(zls.at[c, rows], zlr.at[c, rows], z_pair))
 
     def attended(h, c):
-        direct = (h, c) in DIRECT
-        for m in dmsg[h, c][0 if direct else 1 :] + zmsg[h, c][0 if direct else 2 :]:
+        for m in dmsg[h, c][1:] + zmsg[h, c][2:]:
             m.wait_recv()
-        others = dfm[h, c] + dfp[h, c]
         num = own[h, c] + zfm[h, c].astype(f32) + zfp[h, c].astype(f32)
-        if direct:
-            others = others + dff[DIRECT.index((h, c))]
-            num = num + zff[DIRECT.index((h, c))].astype(f32)
-        den = dn[h, c, 0] + column_of(others)
+        den = dn[h, c, 0] + column_of(dfm[h, c] + dfp[h, c])
         xa[0, h, c] = (num / den).astype(bf16)
         for m in xmsg[h, c]:
             m.start()
 
-    def project_out(c):
-        for h in range(HEADS):
-            for m in xmsg[h, c]:
-                m.wait_recv()
-        rows = jnp.concatenate([xa[r, h, c] for r in range(4) for h in range(HEADS)], axis=1)
-        other = pl.ds(pl.multiple_of((1 - zl) * POS, 128), POS)
-        mine = pl.ds(pl.multiple_of(zl * POS, 128), POS)
-        theirs = wo[:, :, other].reshape(4 * POS, POS)
-        zls[c] = jnp.dot(rows, theirs, preferred_element_type=f32).astype(bf16)
-        zlmsg[c].start()
-        total[c] = jnp.dot(rows, wo[:, :, mine].reshape(4 * POS, POS), preferred_element_type=f32)
-
-    def finish(c):
-        zlmsg[c].wait_recv()
-        mask = jnp.concatenate([lv[0, c * RC : (c + 1) * RC, :].astype(f32)] * (POS // D), axis=1)
-        share = jnp.where(mask > 0.5, total[c] + zlr[c].astype(f32), 0.0)
-        out_ref[c * RC : (c + 1) * RC, :] = share.astype(bf16)
+    def last_attended(p):
+        c, rows = part(p)
+        for m in dmsg[p] + zmsg[p]:
+            m.wait_recv()
+        num = own[LAST, c, rows]
+        for other in (zfm[LAST, c, rows], zfp[LAST, c, rows], zff[c, rows]):
+            num = num + other.astype(f32)
+        others = column_of(dpf[p, 0] + dpf[p, 1] + dpf[p, 2])
+        den = dn[LAST, c, 0, rows] + others[0 : PIECES[p][2], :]
+        xa[0, LAST, c, rows] = (num / den).astype(bf16)
+        for m in xmsg[p]:
+            m.start()
+
+    other_cols = pl.ds(pl.multiple_of((1 - zl) * POS, 128), POS)
+    own_cols = pl.ds(pl.multiple_of(zl * POS, 128), POS)
+
+    split = LAST * D
+
+    def project_early():
+        for h in range(LAST):
+            for c in range(CH):
+                for m in xmsg[h, c]:
+                    m.wait_recv()
+        heads = jnp.concatenate(
+            [xa[r, h].reshape(POS, D) for r in range(4) for h in range(LAST)], axis=1
+        )
+        for cols, acc in ((other_cols, given), (own_cols, total)):
+            weights = wo[:, 0:split, cols].reshape(4 * split, POS)
+            acc[...] = jnp.dot(heads, weights, preferred_element_type=f32).reshape(CH, RC, POS)
+
+    def project_out(p):
+        c, rows = part(p)
+        for m in xmsg[p]:
+            m.wait_recv()
+        heads = jnp.concatenate([xa[r, LAST, c, rows] for r in range(4)], axis=1)
+        theirs = wo[:, split:, other_cols].reshape(4 * D, POS)
+        zls[c, rows] = (given[c, rows] + jnp.dot(heads, theirs, preferred_element_type=f32)).astype(bf16)
+        zlmsg[p].start()
+        mine = wo[:, split:, own_cols].reshape(4 * D, POS)
+        total[c, rows] = total[c, rows] + jnp.dot(heads, mine, preferred_element_type=f32)
+
+    def finish(p):
+        c, rows = part(p)
+        zlmsg[p].wait_recv()
+        first, n = c * RC + PIECES[p][1], PIECES[p][2]
+        mask = jnp.concatenate([lv[0, first : first + n, :].astype(f32)] * (POS // D), axis=1)
+        share = jnp.where(mask > 0.5, total[c, rows] + zlr[c, rows].astype(f32), 0.0)
+        out_ref[first : first + n, :] = share.astype(bf16)
 
     def share_weights():
         for m, share in zip(wo_msg, wo_sib):
             m.wait_recv()
             share.start()
 
-    steps = [(h, c) for h in range(HEADS) for c in range(CH)]
-
-    def step(u):
-        unit(*steps[u], range(4))
-        z_first(*steps[u], slice(0, 4))
+    def step(h, c):
+        unit(h, c, range(4))
+        z_first(h, c, slice(0, 4))
 
     share_near(0)
     forward_q(1)
@@ -378,39 +440,40 @@
     for c in range(CH):
         z_first(0, c, slice(0, 2))
     all_in(1)
-    step(3)
+    step(1, 0)
     share_far(2)
-    step(4)
+    step(1, 1)
     z_relay(0, 0)
     z_relay(0, 1)
     share_weights()
-    step(5)
+    step(1, 2)
     z_relay(0, 2)
     z_relay(1, 0)
     all_in(2)
-    step(6)
+    last_step(0)
     z_relay(1, 1)
-    step(7)
+    last_step(1)
     z_relay(1, 2)
-    step(8)
-    for u in range(6):
-        attended(*steps[u])
+    last_step(2)
+    for h in range(LAST):
+        for c in range(CH):
+            attended(h, c)
     wo_load.wait()
     for m in wo_sib:
         m.wait_recv()
-    attended(*steps[6])
-    attended(*steps[7])
-    project_out(0)
-    attended(*steps[8])
-    project_out(1)
-    project_out(2)
-    for c in range(CH):
-        finish(c)
+    for p in range(len(PIECES)):
+        last_attended(p)
+    project_early()
+    for p in range(len(PIECES)):
+        project_out(p)
+    for p in range(len(PIECES)):
+        finish(p)
     for copy in sent:
         copy.wait_send()
-
-
-MESSAGES = 7 + 6 + 12 + 30 + 54 + 27 - 3 * len(DIRECT) + 27 + 3
+    assert count[0] == MESSAGES
+
+
+MESSAGES = 7 + 6 + 12 + 30 + 54 + 3 * 6 + 18 + 3 * 4
 
 
 def per_device(tokens, survive, norm_gain, w_qkv, qk_gain, w_out):
@@ -418,28 +481,28 @@
     vmem32 = lambda *shape: pltpu.VMEM(shape, f32)
     units = (HEADS, CH)
     scratch = [
+        pltpu.VMEM((CH, RC), jnp.int32), vmem32(1, WIDTH), vmem32(HEADS, 2, D),
         vmem(POS, WIDTH), vmem(POS, WIDTH), vmem(3, WIDTH, POS), vmem(4, POS, 2 * POS),
         vmem(4, HEADS, POS, D), vmem(HEADS, 8, POS, 2 * D), vmem32(8, 8, 128), vmem(8, POS, D),
         vmem32(*units, RC, D), vmem32(*units, 4, RC, D),
         vmem(*units, 3, RC, D), vmem(*units, HALF, D), vmem(*units, HALF, D),
-        vmem(*units, RC, D), vmem(*units, RC, D), vmem(len(DIRECT), RC, D), vmem(*units, 2, HALF, D),
+        vmem(*units, RC, D), vmem(*units, RC, D), vmem(CH, RC, D), vmem(*units, 2, HALF, D),
         vmem32(*units, 3, 1, RC), vmem32(*units, 1, RC), vmem32(*units, 1, RC), vmem32(*units, 1, RC),
-        vmem32(len(DIRECT), 1, RC), vmem32(*units, 1, RC),
-        vmem(4, *units, RC, D), vmem32(CH, RC, POS), vmem(CH, RC, POS), vmem(CH, RC, POS),
-        pltpu.SemaphoreType.DMA((CH + 4,)),
+        vmem32(*units, 1, RC), vmem32(len(PIECES), 3, 1, RC), vmem32(len(PIECES), 3, 1, RC),
+        vmem(4, *units, RC, D), vmem32(CH, RC, POS), vmem32(CH, RC, POS), vmem(CH, RC, POS), vmem(CH, RC, POS),
+        pltpu.SemaphoreType.DMA((CH + 7,)),
         pltpu.SemaphoreType.DMA((MESSAGES,)),
         pltpu.SemaphoreType.DMA((MESSAGES,)),
     ]
     in_hbm = pl.BlockSpec(memory_space=pl.ANY)
-    in_vmem = pl.BlockSpec(memory_space=pltpu.VMEM)
     return pl.pallas_call(
         kernel,
         out_shape=jax.ShapeDtypeStruct((POS, POS), bf16),
-        in_specs=[in_hbm, in_vmem, in_vmem, in_hbm, in_vmem, in_hbm],
-        out_specs=in_vmem,
+        in_specs=[in_hbm] * 6,
+        out_specs=pl.BlockSpec(memory_space=pltpu.VMEM),
         scratch_shapes=scratch,
         compiler_params=pltpu.CompilerParams(
-            collective_id=0, has_side_effects=True, vmem_limit_bytes=60 * 2**20
+            collective_id=0, has_side_effects=True, vmem_limit_bytes=52 * 2**20
         ),
         name="branch",
     )(

time: 78.1 us -> 75.8 us (0.971); the launches traced: 76.6 us -> 75.6 us
  Pallas kernels: 74.9 us -> 72.8 us
  local copies, waits for them, and re-layouts: 1.71 us -> 2.79 us
    pallas_call x1, Pallas kernels: 74.9 us -> 72.8 us  [per_device(): pl.pallas_call(kernel, out_shape=jax.ShapeDtypeStruct((POS, POS), bf16),...]
    unnamed x1 -> x7, local copies, waits for them, and re-layouts: 1.71 us -> 2.79 us
where the time goes in v7:
time: 75.8 us; the launch traced here: 75.6 us
  Pallas kernels  72.8 us (96%)
  local copies, waits for them, and re-layouts  2.79 us (4%)
    pallas_call x1, Pallas kernels, per_device(): pl.pallas_call(kernel, out_shape=jax.ShapeDtypeStruct((POS, POS), bf16),...  72.8 us
    unnamed x7, local copies, waits for them, and re-layouts  2.79 us

profile of v7, /device:TPU:32, one launch (start us, length us, event | category | flops | bytes accessed | tf_op | source)
XLA Modules:
  0.0 75.6 jit_solution(8099287130498457451)
XLA Ops:
  0.0 0.0 copy-start
  0.0 0.7 copy-done
  0.7 0.0 copy-start.1
  0.7 0.7 copy-done.1
  1.4 0.0 copy-start.2
  1.4 0.7 copy-done.2
  2.1 72.8 %branch.1 = bf16[384,384]{1,0:T(8,128)(2,1)S(1)} custom-call(bf16[384,3072]{1,0:T(8,128)(2,1)} %tok_hbm.1, s32[3,128]{1,0:T(4,128)S(1)} %bitcast.6, f32[1,3072]{1,0:T(1,128)S(1)} %bitcast.4, bf16[3,3072,384]{2,1,0:T(8,128)(2,1)} %bitcast.7, f32[3,2,128]{2,1,0:T(2,128)S(1)} %bitcast.5, bf16[384,3072]{1,0:T(8,128)(2,1)} %wo_hbm.1), custom_call_target="tpu_custom_call" | custom-call | tf_op jit(solution)/shard_map/branch/pallas_call | solution.py:498
  74.9 0.7 copy.8
Async XLA Ops:
  0.0 0.7 copy-start
  0.7 0.7 copy-start.1
  1.4 0.7 copy-start.2

commit v8 on v7

--- a/solution.py
+++ b/solution.py
@@ -216,13 +216,10 @@
     send_q(2)
     project_kv(2)
     kv_sib[2][0].start()
-    for m, (_, slot) in zip(live_msg[:3], line[:3]):
-        m.wait_recv()
-        spread_live(slot)
     forward_kv(0)
     send_kv(1, 1)
     send_kv(2, 0)
-    for m, (_, slot) in zip(live_msg[3:], line[3:]):
+    for m, (_, slot) in zip(live_msg, line):
         m.wait_recv()
         spread_live(slot)
 

time: 75.8 us -> 75.8 us (level)
  no operation moved by 1% of the time
where the time goes in v8:
time: 75.8 us; the launch traced here: 75.6 us
  Pallas kernels  72.8 us (96%)
  local copies, waits for them, and re-layouts  2.79 us (4%)
    pallas_call x1, Pallas kernels, per_device(): pl.pallas_call(kernel, out_shape=jax.ShapeDtypeStruct((POS, POS), bf16),...  72.8 us
    unnamed x7, local copies, waits for them, and re-layouts  2.79 us

profile of v8, /device:TPU:32, one launch (start us, length us, event | category | flops | bytes accessed | tf_op | source)
XLA Modules:
  0.0 75.6 jit_solution(525929804414768672)
XLA Ops:
  0.0 0.0 copy-start
  0.0 0.7 copy-done
  0.7 0.0 copy-start.1
  0.7 0.7 copy-done.1
  1.4 0.0 copy-start.2
  1.4 0.7 copy-done.2
  2.1 72.8 %branch.1 = bf16[384,384]{1,0:T(8,128)(2,1)S(1)} custom-call(bf16[384,3072]{1,0:T(8,128)(2,1)} %tok_hbm.1, s32[3,128]{1,0:T(4,128)S(1)} %bitcast.6, f32[1,3072]{1,0:T(1,128)S(1)} %bitcast.4, bf16[3,3072,384]{2,1,0:T(8,128)(2,1)} %bitcast.7, f32[3,2,128]{2,1,0:T(2,128)S(1)} %bitcast.5, bf16[384,3072]{1,0:T(8,128)(2,1)} %wo_hbm.1), custom_call_target="tpu_custom_call" | custom-call | tf_op jit(solution)/shard_map/branch/pallas_call | solution.py:495
  74.9 0.7 copy.8
Async XLA Ops:
  0.0 0.7 copy-start
  0.7 0.7 copy-start.1
  1.4 0.7 copy-start.2
